TPU v7x, 256 devices: a whole 4x4x8 slice. The times are simulated.
256 devices in a mesh: seq: 32 (over z, y_lo, core), tp: 8 (over x, y_hi).
Axes of the slice: x: 4, y: 4 (y_hi: 2, y_lo: 2; y = y_hi * 2 + y_lo), z: 8, core: 2. Of those that a mesh axis runs over, the one named last changes fastest.
Arguments:
- q_raw: bfloat16 [2048, 5120], P('seq', 'tp'), may hold values from -160 to 160
- k_raw: bfloat16 [2048, 5120], P('seq', 'tp'), may hold values from -160 to 160
- v_new: bfloat16 [2048, 5120], P('seq', 'tp'), may hold values from -8 to 8
- q_gain: float32 [5120], P('tp'), may hold values from 1.5 to 3
- k_gain: float32 [5120], P('tp'), may hold values from 1 to 2
- cache_keys: bfloat16 [512, 128, 5120], P('seq', None, 'tp'), may hold values from -10 to 10
- cache_values: bfloat16 [512, 128, 5120], P('seq', None, 'tp'), may hold values from -8 to 8
- page_table: int32 [2, 256], replicated, may hold values from 0 to 511, as said below
- cached_lengths: int32 [2], replicated, may hold values from 6553 to 32768, as said below
- req_group: int32 [8], replicated, may hold values from 0 to 1, as said below
Outputs:
- attended: bfloat16 [2048, 5120], P('seq', 'tp')
Inputs may be any that keep to these rules, and one draw needn't show every extreme that they name: `page_table`: the 256 pages of group g lie on distinct slots s with (s // 8) % 2 == g; every slot holds one page. `cached_lengths`: one group's length is exactly 32768. `req_group`: exactly 4 requests belong to each group.
All inputs are finite; a program needn't handle non-finite values.
Results may differ from a plain program's by a relative error of at most 0.013.
Values may be sent and summed in bfloat16 or wider, within the bound.
No kernel may reach another device: no remote copies, remote signals or barrier semaphores. Data moves between devices by JAX's collectives and lax.ppermute only.
A program may use at most 128 MiB of HBM per device.

v0:
```python
import math

import jax
import jax.numpy as jnp
from jax import lax
from jax.sharding import PartitionSpec as P

HDIM = 128
GROUPS = 2
NEWTOK = 256


EPSILON = 1e-06
MASKED = -1e30


def normalize(raw_rows, gain_row, sum_squares, full_width):
    values = raw_rows.astype(jnp.float32)
    return (
        values * lax.rsqrt(sum_squares[:, None] / full_width + EPSILON) * gain_row[None, :]
    ).astype(jnp.bfloat16)


def on_device(
    q_raw,
    k_raw,
    v_new,
    q_gain,
    k_gain,
    cache_keys,
    cache_values,
    page_table,
    cached_lengths,
    req_group,
):
    tok_dev, width_local = q_raw.shape
    seq_count = lax.axis_size("seq")
    full_width = width_local * lax.axis_size("tp")
    heads_local = width_local // HDIM
    page_len = cache_keys.shape[1]
    pages_dev = cache_keys.shape[0] // GROUPS
    cache_pages = page_table.shape[1]
    requests = req_group.shape[0]
    per_group = requests // GROUPS
    group_tok = per_group * NEWTOK
    seq_index = lax.axis_index("seq")
    raw_query = q_raw.astype(jnp.float32)
    raw_key = k_raw.astype(jnp.float32)
    query_sums, key_sums = lax.psum(
        (jnp.sum(raw_query * raw_query, axis=1), jnp.sum(raw_key * raw_key, axis=1)), "tp"
    )
    queries = normalize(q_raw, q_gain, query_sums, full_width)
    new_keys = normalize(k_raw, k_gain, key_sums, full_width)
    all_queries = lax.all_gather(queries, "seq", axis=0, tiled=True)
    request_ids = jnp.arange(requests, dtype=jnp.int32)
    earlier = (req_group[:, None] == req_group[None, :]) & (
        request_ids[None, :] < request_ids[:, None]
    )
    request_rank = jnp.sum(earlier.astype(jnp.int32), axis=1)
    group_ids = jnp.arange(GROUPS, dtype=jnp.int32)
    rank_ids = jnp.arange(per_group, dtype=jnp.int32)
    chosen = (req_group[None, None, :] == group_ids[:, None, None]) & (
        request_rank[None, None, :] == rank_ids[None, :, None]
    )
    members = jnp.sum(jnp.where(chosen, request_ids[None, None, :], 0), axis=2)
    token_ids = seq_index * tok_dev + jnp.arange(tok_dev, dtype=jnp.int32)
    token_request = token_ids // NEWTOK
    key_layout = cache_keys.reshape(GROUPS, pages_dev * page_len, heads_local, HDIM)
    value_layout = cache_values.reshape(GROUPS, pages_dev * page_len, heads_local, HDIM)
    own_keys = new_keys.reshape(tok_dev, heads_local, HDIM)
    own_values = v_new.reshape(tok_dev, heads_local, HDIM)
    factor = 1.0 / math.sqrt(HDIM)
    offsets = jnp.arange(page_len, dtype=jnp.int32)
    page_ids = jnp.arange(cache_pages, dtype=jnp.int32)
    token_offsets = jnp.arange(NEWTOK, dtype=jnp.int32)
    block_rows = math.gcd(group_tok, 512)
    num_blocks = group_tok // block_rows
    pieces = []
    for group_id in range(GROUPS):
        local_slots = (
            seq_index * (GROUPS * pages_dev)
            + group_id * pages_dev
            + jnp.arange(pages_dev, dtype=jnp.int32)
        )
        matches = page_table[group_id][None, :] == local_slots[:, None]
        logical = jnp.sum(jnp.where(matches, page_ids[None, :], 0), axis=1)
        positions = (logical[:, None] * page_len + offsets[None, :]).reshape(-1)
        usable = positions < cached_lengths[group_id]
        keys_all = jnp.concatenate([key_layout[group_id], own_keys], axis=0)
        values_all = jnp.concatenate([value_layout[group_id], own_values], axis=0)
        query_rows = (members[group_id][:, None] * NEWTOK + token_offsets[None, :]).reshape(-1)
        row_request = jnp.repeat(members[group_id], NEWTOK)
        picked = jnp.take(all_queries, query_rows, axis=0).reshape(
            num_blocks, block_rows, heads_local, HDIM
        )
        picked_request = row_request.reshape(num_blocks, block_rows)

        def attend(operands):
            block_query, block_request = operands
            cached_allowed = jnp.broadcast_to(usable[None, :], (block_rows, usable.shape[0]))
            allowed = jnp.concatenate(
                [cached_allowed, block_request[:, None] == token_request[None, :]], axis=1
            )
            scores = (
                jnp.einsum(
                    "qhd,khd->hqk", block_query, keys_all, preferred_element_type=jnp.float32
                )
                * factor
            )
            scores = jnp.where(allowed[None], scores, MASKED)
            row_top = jnp.max(scores, axis=2)
            weights = jnp.where(allowed[None], jnp.exp(scores - row_top[:, :, None]), 0.0)
            totals = jnp.sum(weights, axis=2)
            mixture = jnp.einsum(
                "hqk,khd->qhd",
                weights.astype(jnp.bfloat16),
                values_all,
                preferred_element_type=jnp.float32,
            )
            return (
                mixture.reshape(block_rows, width_local),
                jnp.transpose(row_top),
                jnp.transpose(totals),
            )

        mixture, row_top, totals = lax.map(attend, (picked, picked_request))
        pieces.append(
            (
                mixture.reshape(group_tok, width_local),
                row_top.reshape(group_tok, heads_local),
                totals.reshape(group_tok, heads_local),
            )
        )
    joined_mix = jnp.concatenate([element[0] for element in pieces], axis=0)
    joined_top = jnp.concatenate([element[1] for element in pieces], axis=0)
    joined_totals = jnp.concatenate([element[2] for element in pieces], axis=0)
    request_base = req_group * group_tok + request_rank * NEWTOK
    placement_rows = (request_base[:, None] + token_offsets[None, :]).reshape(-1)
    token_mix = jnp.take(joined_mix, placement_rows, axis=0)
    token_top = jnp.take(joined_top, placement_rows, axis=0)
    token_totals = jnp.take(joined_totals, placement_rows, axis=0)
    source_mix, source_top, source_totals = (
        lax.all_to_all(
            token_mix.reshape(seq_count, tok_dev, width_local),
            "seq",
            split_axis=0,
            concat_axis=0,
            tiled=True,
        ),
        lax.all_to_all(
            token_top.reshape(seq_count, tok_dev, heads_local),
            "seq",
            split_axis=0,
            concat_axis=0,
            tiled=True,
        ),
        lax.all_to_all(
            token_totals.reshape(seq_count, tok_dev, heads_local),
            "seq",
            split_axis=0,
            concat_axis=0,
            tiled=True,
        ),
    )
    overall = jnp.max(source_top, axis=0)
    scaling = jnp.exp(source_top - overall[None])
    numerator = jnp.sum(
        source_mix.reshape(seq_count, tok_dev, heads_local, HDIM) * scaling[..., None], axis=0
    )
    denominator = jnp.sum(source_totals * scaling, axis=0)
    return (numerator / denominator[..., None]).reshape(tok_dev, width_local).astype(jnp.bfloat16)


def solution(mesh):
    return jax.shard_map(
        on_device,
        mesh=mesh,
        in_specs=(
            P("seq", "tp"),
            P("seq", "tp"),
            P("seq", "tp"),
            P("tp"),
            P("tp"),
            P("seq", None, "tp"),
            P("seq", None, "tp"),
            P(),
            P(),
            P(),
        ),
        out_specs=P("seq", "tp"),
        check_vma=False,
    )
```

profile of v0, /device:TPU:64, one launch (start us, length us, event | category | flops | bytes accessed | tf_op | source)
XLA Modules:
  0.0 388.2 jit_solution(13717035942883513107)
XLA Ops:
  7.6 24.3 %all-reduce = (f32[64]{0:T(128)S(1)}, f32[64]{0:T(128)S(1)}) all-reduce(f32[64]{0:T(128)S(1)} %get-tuple-element.367, f32[64]{0:T(128)S(1)} %get-tuple-element.368), channel_id=1, replica_groups=mesh['seq'=32,'tp'=8] {'tp'}, use_global_device_ids=true, to_apply=%region_2.0 | all-reduce | flops 128 | bytes 1024 | tf_op jit(solution)/shard_map/psum | solution.py:49
  40.4 3.2 squeeze.31
  48.6 2.1 copy.96
  50.9 3.1 fusion.49
  54.0 2.8 copy.93
  56.8 3.2 squeeze.32
  61.9 3.2 squeeze.35
  65.3 3.2 pad_maximum_fusion.4
  68.6 3.6 copy.97
  72.2 2.1 copy.105
  74.5 2.1 copy.106
  80.5 14.9 %all-gather.2.cloned.1.call-done = bf16[2048,640]{1,0:T(8,128)(2,1)} async-done(((bf16[64,640]{1,0:T(8,128)(2,1)}), bf16[2048,640]{1,0:T(8,128)(2,1)}) %all-gather.2.cloned.1.call-update) | async-done | bytes 2621456 | tf_op jit(solution)/shard_map/all_gather | solution.py:54
  95.3 6.3 %gather_fusion.1 = bf16[1024,640]{1,0:T(8,128)(2,1)S(1)} fusion(bf16[2048,640]{1,0:T(8,128)(2,1)} %all-gather.2.cloned.1.call-done, s32[1024]{0:T(1024)S(1)} %fusion.47), kind=kCustom, calls=%fused_computation.clone | custom fusion | bytes 2625536 | tf_op jit(solution)/shard_map/jit(_take)/gather | solution.py:93
  106.4 37.2 %while.30 = (s32[]{:T(128)}, f32[2,512,640]{2,1,0:T(8,128)}, f32[2,512,5]{1,2,0:T(8,128)S(1)}, f32[2,512,5]{1,2,0:T(8,128)S(1)}, s32[2,512]{1,0:T(2,128)S(1)}, /...) while((s32[]{:T(128)}, f32[2,512,640]{2,1,0:T(8,128)}, ...), condition=%wide.region_10.12_spmd.clone, body=%wide.region_7.11_spmd.clone.sunk | while | flops 1462859776 | bytes 45829932 | solution.py:126
  107.8 3.6 fusion.75
  111.4 2.7 fusion.77
  114.1 5.9 %fusion.76 = f32[5,512,128]{1,2,0:T(8,128)} fusion(bf16[1088,5,128]{2,0,1:T(8,128)(2,1)} %get-tuple-element.591, f32[5,512,1088]{1,2,0:T(8,128)S(1)} %get-tuple-element.500, f32[5,512]{1,0:T(8,128)S(1)} %get-tuple-element.501, pred[512,1088]{0,1:T(8,128)(4,1)S(1)} %pad_add_fusion.4), kind=kOutput, calls=%fused_computation.14.clone.1 | convolution fusion | flops 726958080 | bytes 14411776 | tf_op jit(solution)/shard_map/while/body/eval_jaxpr/hqk,khd->qhd/dot_general | solution.py:114
  119.9 2.8 copy.138
  122.7 2.5 constant_dynamic-update-slice_fusion.4
  126.3 3.6 fusion.75
  129.8 2.7 fusion.77
  132.5 5.9 %fusion.76 = f32[5,512,128]{1,2,0:T(8,128)} fusion(bf16[1088,5,128]{2,0,1:T(8,128)(2,1)} %get-tuple-element.591, f32[5,512,1088]{1,2,0:T(8,128)S(1)} %get-tuple-element.500, f32[5,512]{1,0:T(8,128)S(1)} %get-tuple-element.501, pred[512,1088]{0,1:T(8,128)(4,1)S(1)} %pad_add_fusion.4), kind=kOutput, calls=%fused_computation.14.clone.1 | convolution fusion | flops 726958080 | bytes 14411776 | tf_op jit(solution)/shard_map/while/body/eval_jaxpr/hqk,khd->qhd/dot_general | solution.py:114
  138.4 2.8 copy.138
  141.2 2.5 constant_dynamic-update-slice_fusion.4
  143.6 5.2 %gather_fusion.2 = bf16[1024,640]{1,0:T(8,128)(2,1)} fusion(bf16[2048,640]{1,0:T(8,128)(2,1)S(1)} %copy-done, s32[1024]{0:T(1024)S(1)} %fusion.48), kind=kCustom, calls=%fused_computation.2.clone | custom fusion | bytes 2625536 | tf_op jit(solution)/shard_map/jit(_take)/gather | solution.py:93
  150.4 2.5 reshape.314
  152.9 3.1 copy.104
  157.7 31.4 %while.31 = (s32[]{:T(128)}, f32[2,512,640]{2,1,0:T(8,128)}, f32[2,512,5]{1,2,0:T(8,128)S(1)}, f32[2,512,5]{1,2,0:T(8,128)S(1)}, s32[2,512]{1,0:T(2,128)S(1)}, /...) while((s32[]{:T(128)}, f32[2,512,640]{2,1,0:T(8,128)}, ...), condition=%wide.region_15.17_spmd.clone, body=%wide.region_12.16_spmd.clone.sunk | while | flops 1462859776 | bytes 45829932 | solution.py:126
  159.0 3.1 fusion.82
  162.1 2.7 fusion.84
  164.8 5.8 %fusion.83 = f32[5,512,128]{1,2,0:T(8,128)} fusion(bf16[1088,5,128]{2,0,1:T(8,128)(2,1)} %get-tuple-element.552, f32[5,512,1088]{1,2,0:T(8,128)S(1)} %get-tuple-element.515, f32[5,512]{1,0:T(8,128)S(1)} %get-tuple-element.516, pred[512,1088]{0,1:T(8,128)(4,1)S(1)} %pad_add_fusion.5), kind=kOutput, calls=%fused_computation.40.clone.1 | convolution fusion | flops 726958080 | bytes 14411776 | tf_op jit(solution)/shard_map/while/body/eval_jaxpr/hqk,khd->qhd/dot_general | solution.py:114
  174.5 3.1 fusion.82
  177.7 2.7 fusion.84
  180.4 5.8 %fusion.83 = f32[5,512,128]{1,2,0:T(8,128)} fusion(bf16[1088,5,128]{2,0,1:T(8,128)(2,1)} %get-tuple-element.552, f32[5,512,1088]{1,2,0:T(8,128)S(1)} %get-tuple-element.515, f32[5,512]{1,0:T(8,128)S(1)} %get-tuple-element.516, pred[512,1088]{0,1:T(8,128)(4,1)S(1)} %pad_add_fusion.5), kind=kOutput, calls=%fused_computation.40.clone.1 | convolution fusion | flops 726958080 | bytes 14411776 | tf_op jit(solution)/shard_map/while/body/eval_jaxpr/hqk,khd->qhd/dot_general | solution.py:114
  189.9 7.6 %gather_fusion.4 = f32[2048,5]{1,0:T(8,128)} fusion(f32[2048,5]{1,0:T(8,128)S(1)} %copy.111, s32[2048]{0:T(1024)S(1)} %copy-done.4), kind=kCustom, calls=%fused_computation.3.clone | custom fusion | bytes 90112 | tf_op jit(solution)/shard_map/jit(_take)/gather | solution.py:141
  197.4 7.6 %gather_fusion.3 = f32[2048,5]{1,0:T(8,128)} fusion(f32[2048,5]{1,0:T(8,128)S(1)} %copy.108, s32[2048]{0:T(1024)S(1)} %copy-done.4), kind=kCustom, calls=%fused_computation.1.clone | custom fusion | bytes 90112 | tf_op jit(solution)/shard_map/jit(_take)/gather | solution.py:140
  205.0 3.5 broadcast_select_fusion.4
  210.8 7.4 %all-to-all-start.1 = ((f32[32,1,320]{2,1,0:T(1,128)}), f32[32,1,320]{2,1,0:T(1,128)S(1)}, u32[]{:S(2)}, u32[]{:S(2)}) async-start(f32[32,1,320]{2,1,0:T(1,128)} %reshape.329), calls=%async_computation.1 | async-start | bytes 98304 | tf_op jit(solution)/shard_map/all_to_all | solution.py:150
  218.3 4.4 %pad_maximum_fusion = f32[2048,640]{1,0:T(8,128)} fusion(f32[1024,640]{1,0:T(8,128)S(1)} %bitcast.133, f32[1024,640]{1,0:T(8,128)} %bitcast.134), kind=kLoop, calls=%fused_computation.61 | loop fusion | flops 1310720 | bytes 10485760 | tf_op jit(solution)/shard_map/concatenate | solution.py:134
  225.0 12.4 %gather_fusion = f32[2048,640]{1,0:T(8,128)} fusion(f32[2048,640]{1,0:T(8,128)} %pad_maximum_fusion, s32[2048]{0:T(1024)S(1)} %copy-done.5), kind=kCustom, calls=%fused_computation.4 | custom fusion | bytes 10493952 | tf_op jit(solution)/shard_map/jit(_take)/gather | solution.py:139
  237.5 8.3 %all-to-all-start.2 = ((f32[32,1,320]{2,1,0:T(1,128)}), f32[32,1,320]{2,1,0:T(1,128)S(1)}, u32[]{:S(2)}, u32[]{:S(2)}) async-start(f32[32,1,320]{2,1,0:T(1,128)} %reshape.331), calls=%async_computation.2 | async-start | bytes 98304 | tf_op jit(solution)/shard_map/all_to_all | solution.py:157
  245.8 4.4 %broadcast_select_fusion = f32[32,64,640]{2,1,0:T(8,128)} fusion(f32[32,64,640]{2,1,0:T(8,128)} %bitcast.132, pred[32,64]{1,0:T(8,128)(4,1)S(1)} %copy-done.6), kind=kLoop, calls=%fused_computation.63 | loop fusion | flops 1310720 | bytes 10487808 | tf_op jit(solution)/shard_map/jit(_take)/select_n | solution.py:139
  250.1 2.2 all-to-all-done.2
  252.3 6.5 %all-to-all-start = ((f32[32,64,640]{2,1,0:T(8,128)}), f32[32,64,640]{2,1,0:T(8,128)}, u32[]{:S(2)}, u32[]{:S(2)}) async-start(f32[32,64,640]{2,1,0:T(8,128)} %broadcast_select_fusion), calls=%async_computation | async-start | bytes 10485760 | tf_op jit(solution)/shard_map/all_to_all | solution.py:143
  261.5 4.6 %mul.129 = f32[32,64,5,128]{3,2,1,0:T(8,128)} broadcast(f32[32,64,5]{2,1,0:T(8,128)S(1)} %copy.110), dimensions={0,1,2} | broadcast | bytes 5283840 | tf_op jit(solution)/shard_map/mul | solution.py:168
  266.1 8.3 %mul.130 = f32[32,64,640]{2,1,0:T(8,128)} reshape(f32[32,64,5,128]{3,2,1,0:T(8,128)} %mul.129) | data formatting | bytes 10485760 | tf_op jit(solution)/shard_map/mul | solution.py:168
  274.4 101.6 %all-to-all-done = f32[32,64,640]{2,1,0:T(8,128)} async-done(((f32[32,64,640]{2,1,0:T(8,128)}), f32[32,64,640]{2,1,0:T(8,128)}, u32[]{:S(2)}, u32[]{:S(2)}) %all-to-all-start) | async-done | bytes 5242912 | tf_op jit(solution)/shard_map/all_to_all | solution.py:143
  376.0 4.6 %multiply_reduce_fusion = f32[64,640]{1,0:T(8,128)S(1)} fusion(f32[32,64,640]{2,1,0:T(8,128)} %all-to-all-done, f32[32,64,640]{2,1,0:T(8,128)} %mul.130), kind=kLoop, calls=%fused_computation.62 | loop fusion | flops 2580480 | bytes 10649600 | tf_op jit(solution)/shard_map/reduce_sum | solution.py:167
  (138 shorter events, 47.8 us)
Async XLA Ops:
  6.5 88.8 %all-gather.2.cloned.1.call-start = ((), (), s32[]{:S(2)}) async-start(), calls=%async_computation.3 | async-start | bytes 2703360 | tf_op jit(solution)/shard_map/all_gather | solution.py:54
  60.1 5.1 %copy-start.3 = (bf16[64,640]{1,0:T(8,128)(2,1)S(1)}, bf16[64,640]{1,0:T(8,128)(2,1)}, u32[]{:S(2)}) copy-start(bf16[64,640]{1,0:T(8,128)(2,1)} %param.20) | copy-start | bytes 245764
  72.2 4.4 %copy-start.10 = (s32[8]{0:T(128)S(1)}, s32[8]{0:T(128)}, u32[]{:S(2)}) copy-start(s32[8]{0:T(128)} %param.27) | copy-start | bytes 100
  72.2 4.7 %copy-start.9 = (s32[2]{0:T(128)S(1)}, s32[2]{0:T(128)}, u32[]{:S(2)}) copy-start(s32[2]{0:T(128)} %param.26) | copy-start | bytes 28
  72.2 5.4 %copy-start.8 = (s32[2,256]{1,0:T(2,128)S(1)}, s32[2,256]{1,0:T(2,128)}, u32[]{:S(2)}) copy-start(s32[2,256]{1,0:T(2,128)} %param.25) | copy-start | bytes 6148
  106.4 37.2 %copy-start = (bf16[2048,640]{1,0:T(8,128)(2,1)S(1)}, bf16[2048,640]{1,0:T(8,128)(2,1)}, u32[]{:S(2)}) copy-start(bf16[2048,640]{1,0:T(8,128)(2,1)} %all-gather.2.cloned.1.call-done) | copy-start | bytes 7864324
  152.9 4.8 %copy-start.1 = (bf16[1088,5,128]{2,0,1:T(8,128)(2,1)S(1)}, bf16[1088,5,128]{2,0,1:T(8,128)(2,1)}, u32[]{:S(2)}) copy-start(bf16[1088,5,128]{2,0,1:T(8,128)(2,1)} %copy.105) | copy-start | bytes 4177924
  157.6 32.2 %copy-start.4 = (s32[2048]{0:T(1024)S(1)}, s32[2048]{0:T(1024)}, u32[]{:S(2)}) copy-start(s32[2048]{0:T(1024)} %fusion.45) | copy-start | bytes 24580
  197.4 7.6 %copy-start.7 = (pred[2048]{0:T(1024)(128)(4,1)S(1)}, pred[2048]{0:T(1024)(128)(4,1)}, u32[]{:S(2)}) copy-start(pred[2048]{0:T(1024)(128)(4,1)} %compare_and_fusion.1) | copy-start | bytes 6148
  205.0 13.3 %copy-start.2 = (f32[2,512,640]{2,1,0:T(8,128)S(1)}, f32[2,512,640]{2,1,0:T(8,128)}, u32[]{:S(2)}) copy-start(f32[2,512,640]{2,1,0:T(8,128)} %get-tuple-element.116) | copy-start | bytes 7864324
  210.8 26.6 %all-to-all-start.1 = ((f32[32,1,320]{2,1,0:T(1,128)}), f32[32,1,320]{2,1,0:T(1,128)S(1)}, u32[]{:S(2)}, u32[]{:S(2)}) async-start(f32[32,1,320]{2,1,0:T(1,128)} %reshape.329), calls=%async_computation.1 | async-start | bytes 98304 | tf_op jit(solution)/shard_map/all_to_all | solution.py:150
  218.3 6.7 %copy-start.5 = (s32[2048]{0:T(1024)S(1)}, s32[2048]{0:T(1024)}, u32[]{:S(2)}) copy-start(s32[2048]{0:T(1024)} %broadcast_clamp_fusion) | copy-start | bytes 24580
  225.0 20.7 %copy-start.6 = (pred[32,64]{1,0:T(8,128)(4,1)S(1)}, pred[32,64]{1,0:T(8,128)(4,1)}, u32[]{:S(2)}) copy-start(pred[32,64]{1,0:T(8,128)(4,1)} %compare_and_fusion) | copy-start | bytes 6148
  237.5 14.8 %all-to-all-start.2 = ((f32[32,1,320]{2,1,0:T(1,128)}), f32[32,1,320]{2,1,0:T(1,128)S(1)}, u32[]{:S(2)}, u32[]{:S(2)}) async-start(f32[32,1,320]{2,1,0:T(1,128)} %reshape.331), calls=%async_computation.2 | async-start | bytes 98304 | tf_op jit(solution)/shard_map/all_to_all | solution.py:157
  252.3 123.7 %all-to-all-start = ((f32[32,64,640]{2,1,0:T(8,128)}), f32[32,64,640]{2,1,0:T(8,128)}, u32[]{:S(2)}, u32[]{:S(2)}) async-start(f32[32,64,640]{2,1,0:T(8,128)} %broadcast_select_fusion), calls=%async_computation | async-start | bytes 10485760 | tf_op jit(solution)/shard_map/all_to_all | solution.py:143
Sparse Core Ops, SparseCore 0:
  33.7 61.5 all-gather.1
where the time goes:
time: 393 us; the launch traced here: 388 us
  local copies, waits for them, and re-layouts  122 us (31%)
  waiting for transfers between devices  119 us (30%)
  other arithmetic  49.6 us (13%)
  matrix products  36.8 us (9%)
  blocking collectives  24.3 us (6%)
  starting transfers between devices  22.2 us (6%)
  between operations  13.7 us (3%)
    all_to_all x1, waiting for transfers between devices, on_device(): lax.all_to_all(token_mix.reshape(seq_count, tok_dev, width_local), 'seq',...  102 us
    psum x1, blocking collectives, on_device(): lax.psum((jnp.sum(raw_query * raw_query, axis=1), jnp.sum(raw_key * raw_k...  24.3 us
    dot_general x4, matrix products, attend(): jnp.einsum('hqk,khd->qhd', weights.astype(jnp.bfloat16), values_all, pref...  23.4 us
    dynamic_update_slice x12, local copies, waits for them, and re-layouts, on_device(): mixture, row_top, totals = lax.map(attend, (picked, picked_request))  16.3 us
    unnamed x40, local copies, waits for them, and re-layouts  16.2 us
    all_gather x1, waiting for transfers between devices, on_device(): all_queries = lax.all_gather(queries, 'seq', axis=0, tiled=True)  14.9 us
    dot_general x4, matrix products, attend(): jnp.einsum('qhd,khd->hqk', block_query, keys_all, preferred_element_type=...  13.4 us
    mul x2, local copies, waits for them, and re-layouts, on_device(): source_mix.reshape(seq_count, tok_dev, heads_local, HDIM)  12.8 us
  transfers between devices with their start and end apart: 4, of which 3 were waited for; matrix products, arithmetic and copies ran while one was open for 22% of the time, Pallas kernels for 0%

commit v1 on v0

v1 whole, which is shorter than its diff:
```python
import functools
import math

import jax
import jax.numpy as jnp
from jax import lax
from jax.experimental import pallas as pl
from jax.experimental.pallas import tpu as pltpu
from jax.sharding import PartitionSpec as P

HDIM = 128
GROUPS = 2
NEWTOK = 256
EPSILON = 1e-06
MASKED = -1e30
STAT_ROWS = 8


def pieces(values):
    high = values.astype(jnp.bfloat16)
    rest = values - high.astype(jnp.float32)
    middle = rest.astype(jnp.bfloat16)
    low = (rest - middle.astype(jnp.float32)).astype(jnp.bfloat16)
    return high, middle, low


def to_columns(rows):
    count = rows.shape[0]
    if count < 128:
        rows = jnp.concatenate([rows, jnp.zeros((128 - count, 128), jnp.float32)], axis=0)
    return rows.T


def sums_kernel(q_ref, k_ref, out_ref):
    tokens = q_ref.shape[0]
    query = q_ref[...].astype(jnp.float32)
    key = k_ref[...].astype(jnp.float32)
    query_sum = jnp.sum(query * query, axis=1, keepdims=True)
    key_sum = jnp.sum(key * key, axis=1, keepdims=True)
    lane = lax.broadcasted_iota(jnp.int32, (tokens, 128), 1)
    both = jnp.where(lane == 0, query_sum, jnp.where(lane == 1, key_sum, 0.0))
    padded = jnp.concatenate([both, jnp.zeros((128 - tokens, 128), jnp.float32)], axis=0)
    rows = padded.T[0:8]
    for index in range(out_ref.shape[0]):
        out_ref[index] = rows


def norm_kernel(q_ref, k_ref, v_ref, qg_ref, kg_ref, sums_ref, q_out, k_out, v_out, *, full_width, scale):
    tokens, width = q_ref.shape
    total = sums_ref[0]
    for index in range(1, sums_ref.shape[0]):
        total = total + sums_ref[index]
    inverse = to_columns(lax.rsqrt(total / full_width + EPSILON))
    query_inverse = inverse[0:tokens, 0:1]
    key_inverse = inverse[0:tokens, 1:2]
    q_out[...] = (
        q_ref[...].astype(jnp.float32) * query_inverse * (qg_ref[...] * scale)
    ).astype(jnp.bfloat16)
    k_out[0:tokens] = (
        k_ref[...].astype(jnp.float32) * key_inverse * kg_ref[...]
    ).astype(jnp.bfloat16)
    v_out[0:tokens] = v_ref[...]
    blank = jnp.zeros((k_out.shape[0] - tokens, width), jnp.bfloat16)
    k_out[tokens:] = blank
    v_out[tokens:] = blank


def attend_kernel(
    group_ref,
    length_ref,
    place_ref,
    table_ref,
    qa_ref,
    qb_ref,
    key_ref,
    value_ref,
    own_key_ref,
    own_value_ref,
    oa_ref,
    ob_ref,
    bias_ref,
    *,
    heads,
    pages,
    page_len,
    tok_dev,
):
    request = pl.program_id(0)
    group = group_ref[request]
    seq_index = place_ref[0]
    own_request = place_ref[1]
    cached = pages * page_len
    own_rows = own_key_ref.shape[0]

    @pl.when(request == 0)
    def _():
        lane = lax.broadcasted_iota(jnp.int32, (1, page_len), 1)
        page_ids = lax.broadcasted_iota(jnp.int32, (1, table_ref.shape[1]), 1)
        for group_id in range(GROUPS):
            table_row = table_ref[group_id : group_id + 1, :]
            for page in range(pages):
                slot = seq_index * (GROUPS * pages) + group_id * pages + page
                logical = jnp.sum(
                    jnp.where(table_row == slot, page_ids, 0), axis=1, keepdims=True
                )
                usable = logical * page_len + lane < length_ref[group_id]
                bias_ref[group_id, 0:1, page * page_len : (page + 1) * page_len] = jnp.where(
                    usable, 0.0, MASKED
                )

    def body(masked):
        if masked:
            own_lane = lax.broadcasted_iota(jnp.int32, (1, own_rows), 1)
            limit = jnp.where(request == own_request, tok_dev, 0)
            own_bias = jnp.where(own_lane < limit, 0.0, MASKED)
        for q_ref, o_ref in ((qa_ref, oa_ref), (qb_ref, ob_ref)):
            rows = q_ref.shape[1]
            lane = lax.broadcasted_iota(jnp.int32, (rows, 128), 1)
            stats = jnp.zeros((rows, 128), jnp.float32)
            for head in range(heads):
                columns = slice(head * HDIM, (head + 1) * HDIM)
                query = q_ref[0, :, columns]
                keys = key_ref[pl.ds(group * pages, pages), :, columns].reshape(cached, HDIM)
                values = value_ref[pl.ds(group * pages, pages), :, columns].reshape(cached, HDIM)
                scores = lax.dot_general(
                    query, keys, (((1,), (1,)), ((), ())), preferred_element_type=jnp.float32
                )
                if masked:
                    scores = scores + bias_ref[group]
                    own_scores = lax.dot_general(
                        query,
                        own_key_ref[:, columns],
                        (((1,), (1,)), ((), ())),
                        preferred_element_type=jnp.float32,
                    )
                    own_scores = own_scores + own_bias
                top = jnp.max(scores, axis=1, keepdims=True)
                if masked:
                    top = jnp.maximum(top, jnp.max(own_scores, axis=1, keepdims=True))
                weights = jnp.exp2(scores - top)
                total = jnp.sum(weights, axis=1, keepdims=True)
                mixed = jnp.dot(
                    weights.astype(jnp.bfloat16), values, preferred_element_type=jnp.float32
                )
                if masked:
                    own_weights = jnp.exp2(own_scores - top)
                    total = total + jnp.sum(own_weights, axis=1, keepdims=True)
                    mixed = mixed + jnp.dot(
                        own_weights.astype(jnp.bfloat16),
                        own_value_ref[:, columns],
                        preferred_element_type=jnp.float32,
                    )
                o_ref[0, 0:rows, columns] = (mixed * (1.0 / total)).astype(jnp.bfloat16)
                stats = jnp.where(lane == head, top + jnp.log2(total), stats)
            write_stats(o_ref, stats.T[0:STAT_ROWS], rows)

    plain = (length_ref[group] == table_ref.shape[1] * page_len) & (request != own_request)

    @pl.when(plain)
    def _():
        body(False)

    @pl.when(jnp.logical_not(plain))
    def _():
        body(True)


def write_stats(o_ref, stats, rows):
    for index, piece in enumerate(pieces(stats)):
        o_ref[0, rows : rows + STAT_ROWS, index * 128 : (index + 1) * 128] = piece
    left = o_ref.shape[2] - 3 * 128
    o_ref[0, rows : rows + STAT_ROWS, 3 * 128 :] = jnp.zeros((STAT_ROWS, left), jnp.bfloat16)


def read_stats(block, rows):
    stats = block[rows : rows + STAT_ROWS, 0:384].astype(jnp.float32)
    return stats[:, 0:128] + stats[:, 128:256] + stats[:, 256:384]


def pair_kernel(a_ref, b_ref, out_ref, *, heads):
    rows = a_ref.shape[1] - STAT_ROWS
    stat_a = read_stats(a_ref.at[0], rows)
    stat_b = read_stats(b_ref.at[0], rows)
    top = jnp.maximum(stat_a, stat_b)
    weight_a = jnp.exp2(stat_a - top)
    weight_b = jnp.exp2(stat_b - top)
    total = weight_a + weight_b
    factors = to_columns(jnp.concatenate([weight_a / total, weight_b / total], axis=0))
    for head in range(heads):
        columns = slice(head * HDIM, (head + 1) * HDIM)
        out_ref[0, 0:rows, columns] = (
            a_ref[0, 0:rows, columns].astype(jnp.float32) * factors[:, head : head + 1]
            + b_ref[0, 0:rows, columns].astype(jnp.float32)
            * factors[:, STAT_ROWS + head : STAT_ROWS + head + 1]
        ).astype(jnp.bfloat16)
    write_stats(out_ref, top + jnp.log2(total), rows)


def many_kernel(in_ref, keep_ref, send_ref, *, heads):
    count = in_ref.shape[0]
    rows = in_ref.shape[1] - STAT_ROWS
    half = rows // 2
    stats = [read_stats(in_ref.at[index], rows) for index in range(count)]
    top = functools.reduce(jnp.maximum, stats)
    weights = [jnp.exp2(stat - top) for stat in stats]
    total = functools.reduce(jnp.add, weights)
    factors = to_columns(jnp.concatenate([weight / total for weight in weights], axis=0))
    for head in range(heads):
        columns = slice(head * HDIM, (head + 1) * HDIM)
        merged = None
        for index in range(count):
            lane = index * STAT_ROWS + head
            term = in_ref[index, 0:rows, columns].astype(jnp.float32) * factors[:, lane : lane + 1]
            merged = term if merged is None else merged + term
        merged = merged.astype(jnp.bfloat16)
        keep_ref[0, 0:half, columns] = merged[0:half]
        send_ref[0, 0:half, columns] = merged[half:]
    stat = top + jnp.log2(total)
    write_stats(keep_ref, stat, half)
    swapped = jnp.concatenate([stat[:, half:], stat[:, 0:half]], axis=1)
    write_stats(send_ref, swapped, half)


def last_kernel(a_ref, b_ref, out_ref, *, heads):
    rows = out_ref.shape[0]
    stat_a = read_stats(a_ref.at[0], rows)
    stat_b = read_stats(b_ref.at[0], rows)
    top = jnp.maximum(stat_a, stat_b)
    weight_a = jnp.exp2(stat_a - top)
    weight_b = jnp.exp2(stat_b - top)
    total = weight_a + weight_b
    factors = to_columns(jnp.concatenate([weight_a / total, weight_b / total], axis=0))[0:rows]
    for head in range(heads):
        columns = slice(head * HDIM, (head + 1) * HDIM)
        out_ref[:, columns] = (
            a_ref[0, 0:rows, columns].astype(jnp.float32) * factors[:, head : head + 1]
            + b_ref[0, 0:rows, columns].astype(jnp.float32)
            * factors[:, STAT_ROWS + head : STAT_ROWS + head + 1]
        ).astype(jnp.bfloat16)


def on_device(
    q_raw,
    k_raw,
    v_new,
    q_gain,
    k_gain,
    cache_keys,
    cache_values,
    page_table,
    cached_lengths,
    req_group,
):
    tok_dev, width = q_raw.shape
    tp_count = lax.axis_size("tp")
    seq_count = lax.axis_size("seq")
    heads = width // HDIM
    page_len = cache_keys.shape[1]
    pages = cache_keys.shape[0] // GROUPS
    requests = req_group.shape[0]
    plane = seq_count // requests
    seq_index = lax.axis_index("seq")
    bf16 = jnp.bfloat16
    f32 = jnp.float32
    scale = math.log2(math.e) / math.sqrt(HDIM)
    z_groups = [[z * plane + member for z in range(requests)] for member in range(plane)]
    core_pairs = [(index, index ^ 1) for index in range(seq_count)]
    y_pairs = [(index, index ^ 2) for index in range(seq_count)]

    sums = pl.pallas_call(
        sums_kernel, out_shape=jax.ShapeDtypeStruct((tp_count, 8, 128), f32), name="sums"
    )(q_raw, k_raw)
    sums = lax.all_to_all(sums, "tp", split_axis=0, concat_axis=0, tiled=True)
    queries, own_keys, own_values = pl.pallas_call(
        functools.partial(norm_kernel, full_width=float(width * tp_count), scale=scale),
        out_shape=(
            jax.ShapeDtypeStruct((tok_dev, width), bf16),
            jax.ShapeDtypeStruct((128, width), bf16),
            jax.ShapeDtypeStruct((128, width), bf16),
        ),
        name="norm",
    )(q_raw, k_raw, v_new, q_gain[None, :], k_gain[None, :], sums)

    other = lax.ppermute(queries, "seq", y_pairs)
    rows = 2 * tok_dev
    mine = jnp.concatenate([queries, other], axis=0)
    spread = jnp.broadcast_to(mine[None], (requests, rows, width))
    queries_a = lax.all_to_all(
        spread, "seq", split_axis=0, concat_axis=0, tiled=True, axis_index_groups=z_groups
    )
    queries_b = lax.ppermute(queries_a, "seq", core_pairs)

    chunk = rows + STAT_ROWS
    place = jnp.stack([seq_index, seq_index // plane]).astype(jnp.int32)
    block_q = pl.BlockSpec((1, rows, width), lambda r, *_: (r, 0, 0))
    block_o = pl.BlockSpec((1, chunk, width), lambda r, *_: (r, 0, 0))
    whole = lambda array: pl.BlockSpec(array.shape, lambda r, *_: (0,) * array.ndim)
    partial_shape = jax.ShapeDtypeStruct((requests, chunk, width), bf16)
    out_a, out_b = pl.pallas_call(
        functools.partial(
            attend_kernel, heads=heads, pages=pages, page_len=page_len, tok_dev=tok_dev
        ),
        out_shape=(partial_shape, partial_shape),
        grid_spec=pltpu.PrefetchScalarGridSpec(
            num_scalar_prefetch=3,
            grid=(requests,),
            in_specs=[
                whole(page_table),
                block_q,
                block_q,
                whole(cache_keys),
                whole(cache_values),
                whole(own_keys),
                whole(own_values),
            ],
            out_specs=(block_o, block_o),
            scratch_shapes=[pltpu.VMEM((GROUPS, 1, pages * page_len), f32)],
        ),
        name="attend",
    )(
        req_group,
        cached_lengths,
        place,
        page_table,
        queries_a,
        queries_b,
        cache_keys,
        cache_values,
        own_keys,
        own_values,
    )

    out_b = lax.ppermute(out_b, "seq", core_pairs)
    merged = pl.pallas_call(
        functools.partial(pair_kernel, heads=heads),
        out_shape=partial_shape,
        grid=(requests,),
        in_specs=[pl.BlockSpec((1, chunk, width), lambda r: (r, 0, 0))] * 2,
        out_specs=pl.BlockSpec((1, chunk, width), lambda r: (r, 0, 0)),
        name="pair",
    )(out_a, out_b)
    merged = lax.all_to_all(
        merged, "seq", split_axis=0, concat_axis=0, tiled=True, axis_index_groups=z_groups
    )
    small = jax.ShapeDtypeStruct((1, tok_dev + STAT_ROWS, width), bf16)
    keep, send = pl.pallas_call(
        functools.partial(many_kernel, heads=heads), out_shape=(small, small), name="many"
    )(merged)
    send = lax.ppermute(send, "seq", y_pairs)
    return pl.pallas_call(
        functools.partial(last_kernel, heads=heads),
        out_shape=jax.ShapeDtypeStruct((tok_dev, width), bf16),
        name="last",
    )(keep, send)


def solution(mesh):
    return jax.shard_map(
        on_device,
        mesh=mesh,
        in_specs=(
            P("seq", "tp"),
            P("seq", "tp"),
            P("seq", "tp"),
            P("tp"),
            P("tp"),
            P("seq", None, "tp"),
            P("seq", None, "tp"),
            P(),
            P(),
            P(),
        ),
        out_specs=P("seq", "tp"),
        check_vma=False,
    )
```

time: 393 us -> 167 us (0.42)
  local copies, waits for them, and re-layouts: 122 us -> 6.02 us
  waiting for transfers between devices: 119 us -> 18.8 us
  blocking collectives: 24.3 us -> 78.5 us
  Pallas kernels: 0 us -> 50.7 us
  other arithmetic: 49.6 us -> 1.65 us
  matrix products: 36.8 us -> 0 us
  starting transfers between devices: 22.2 us -> 8.43 us
  between operations: 13.7 us -> 0.03 us
    all_to_all x3 -> x1, waiting for transfers between devices: 104 us -> 5.19 us  [on_device(): sums = lax.all_to_all(sums, 'tp', split_axis=0, concat_axis=0, tiled=True)]
    all_to_all x0 -> x2, blocking collectives: none -> 78.5 us  [the longest x1 41.5 us: on_device(): lax.all_to_all(merged, 'seq', split_axis=0, concat_axis=0, tiled=True, ax...]
    pallas_call x0 -> x6, Pallas kernels: none -> 50.7 us  [the longest x1 35.1 us: on_device(): pl.pallas_call(functools.partial(attend_kernel, heads=heads, pages=pages,...]
    gather x5 -> x0, local copies, waits for them, and re-layouts: 39 us -> none  [the longest x1 12.4 us: on_device(): token_mix = jnp.take(joined_mix, placement_rows, axis=0)]
    dot_general x8 -> x0, matrix products: 36.8 us -> none  [the longest x4 23.4 us: attend(): jnp.einsum('hqk,khd->qhd', weights.astype(jnp.bfloat16), values_all, pref...]
    psum x1 -> x0, blocking collectives: 24.3 us -> none  [on_device(): lax.psum((jnp.sum(raw_query * raw_query, axis=1), jnp.sum(raw_key * raw_k...]
    reduce_sum x11 -> x0, other arithmetic: 17.8 us -> none  [the longest x4 10.7 us: attend(): totals = jnp.sum(weights, axis=2)]
    dynamic_update_slice x12 -> x0, local copies, waits for them, and re-layouts: 16.3 us -> none  [on_device(): mixture, row_top, totals = lax.map(attend, (picked, picked_request))]
  transfers between devices with their start and end apart: 4 -> 5, of which waited for: 3 -> 5; matrix products, arithmetic and copies ran while one was open for 22% -> 2% of each run, Pallas kernels for 0% -> 0%
where the time goes in v1:
time: 167 us; the launch traced here: 164 us
  blocking collectives  78.5 us (47%)
  Pallas kernels  50.7 us (30%)
  waiting for transfers between devices  18.8 us (11%)
  starting transfers between devices  8.43 us (5%)
  local copies, waits for them, and re-layouts  6.02 us (4%)
    all_to_all x1, blocking collectives, on_device(): lax.all_to_all(merged, 'seq', split_axis=0, concat_axis=0, tiled=True, ax...  41.5 us
    all_to_all x1, blocking collectives, on_device(): lax.all_to_all(spread, 'seq', split_axis=0, concat_axis=0, tiled=True, ax...  37 us
    pallas_call x1, Pallas kernels, on_device(): pl.pallas_call(functools.partial(attend_kernel, heads=heads, pages=pages,...  35.1 us
    pallas_call x1, Pallas kernels, on_device(): pl.pallas_call(functools.partial(pair_kernel, heads=heads), out_shape=par...  7.17 us
    all_to_all x1, starting transfers between devices, on_device(): sums = lax.all_to_all(sums, 'tp', split_axis=0, concat_axis=0, tiled=True)  6.93 us
    all_to_all x1, waiting for transfers between devices, on_device(): sums = lax.all_to_all(sums, 'tp', split_axis=0, concat_axis=0, tiled=True)  5.19 us
    ppermute x1, waiting for transfers between devices, on_device(): send = lax.ppermute(send, 'seq', y_pairs)  4.08 us
    ppermute x1, waiting for transfers between devices, on_device(): other = lax.ppermute(queries, 'seq', y_pairs)  3.97 us
  transfers between devices with their start and end apart: 5, of which 5 were waited for; matrix products, arithmetic and copies ran while one was open for 2% of the time, Pallas kernels for 0%

profile of v1, /device:TPU:64, one launch (start us, length us, event | category | flops | bytes accessed | tf_op | source)
XLA Modules:
  0.0 164.1 jit_solution(1667774798604539291)
XLA Ops:
  0.0 1.7 %sums.1 = f32[8,8,128]{2,1,0:T(8,128)} custom-call(bf16[64,640]{1,0:T(8,128)(2,1)} %q_ref.3, bf16[64,640]{1,0:T(8,128)(2,1)} %k_ref.3), custom_call_target="tpu_custom_call" | custom-call | tf_op jit(solution)/shard_map/sums/pallas_call | solution.py:270
  1.7 6.9 %all-to-all-start = ((f32[8,8,128]{2,1,0:T(8,128)}), f32[8,8,128]{2,1,0:T(8,128)S(1)}, u32[]{:S(2)}, u32[]{:S(2)}) async-start(f32[8,8,128]{2,1,0:T(8,128)} %sums.1), calls=%async_computation | async-start | bytes 65536 | tf_op jit(solution)/shard_map/all_to_all | solution.py:273
  8.6 1.3 broadcast_in_dim.12.qg_ref
  9.9 1.3 broadcast_in_dim.13.kg_ref
  11.2 5.2 %all-to-all-done.sums_ref = f32[8,8,128]{2,1,0:T(8,128)S(1)} async-done(((f32[8,8,128]{2,1,0:T(8,128)}), f32[8,8,128]{2,1,0:T(8,128)S(1)}, u32[]{:S(2)}, u32[]{:S(2)}) %all-to-all-start) | async-done | bytes 32800 | tf_op jit(solution)/shard_map/all_to_all | solution.py:273
  16.4 0.0 copy-start.3
  16.4 0.6 copy-done.3
  17.0 1.9 %norm.1 = (bf16[64,640]{1,0:T(8,128)(2,1)}, bf16[128,640]{1,0:T(8,128)(2,1)}, bf16[128,640]{1,0:T(8,128)(2,1)}) custom-call(bf16[64,640]{1,0:T(8,128)(2,1)} %q_ref.3, bf16[64,640]{1,0:T(8,128)(2,1)} %k_ref.3, bf16[64,640]{1,0:T(8,128)(2,1)} %v_ref.1, f32[1,640]{1,0:T(1,128)} %broadcast_in_dim.12.qg_ref, f32[1,640]{1,0:T(1,128)} %broadcast_in_dim.13.kg_ref, ...), custom_call_target="tpu_custom_call" | custom-call | tf_op jit(solution)/shard_map/norm/pallas_call | solution.py:274
  18.9 0.7 collective-permute-start
  19.5 4.0 %collective-permute-done = bf16[64,640]{1,0:T(8,128)(2,1)S(1)} collective-permute-done((bf16[64,640]{1,0:T(8,128)(2,1)}, bf16[64,640]{1,0:T(8,128)(2,1)S(1)}, u32[]{:S(2)}, u32[]{:S(2)}) %collective-permute-start) | collective-permute-done | bytes 81952 | tf_op jit(solution)/shard_map/ppermute | solution.py:284
  23.5 0.9 pad_maximum_fusion
  24.4 0.1 broadcast_in_dim.14
  24.5 37.0 %all_to_all.15.qa_ref = bf16[8,128,640]{2,1,0:T(8,128)(2,1)S(1)} all-to-all(bf16[8,128,640]{2,1,0:T(8,128)(2,1)S(1)} %broadcast_in_dim.14), channel_id=1, replica_groups={{0,32,64,96,128,160,192,224},{8,40,72,104,136,168,200,232},{16,48,80,11..., dimensions={0} | all-to-all | bytes 2621440 | tf_op jit(solution)/shard_map/all_to_all | solution.py:288
  61.6 0.0 copy-start
  61.6 0.0 collective-permute-start.1
  61.6 0.7 pad_add_fusion.place_ref
  62.3 2.3 %collective-permute-done.1.qb_ref = bf16[8,128,640]{2,1,0:T(8,128)(2,1)S(1)} collective-permute-done((bf16[8,128,640]{2,1,0:T(8,128)(2,1)S(1)}, bf16[8,128,640]{2,1,0:T(8,128)(2,1)S(1)}, u32[]{:S(2)}, u32[]{:S(2)}) %collective-permute-start.1) | collective-permute-done | bytes 1310752 | tf_op jit(solution)/shard_map/ppermute | solution.py:291
  64.6 0.0 copy-start.2
  64.6 0.0 copy-done
  64.6 1.1 copy-done.2
  65.7 35.1 %attend.1 = (bf16[8,136,640]{2,1,0:T(8,128)(2,1)}, bf16[8,136,640]{2,1,0:T(8,128)(2,1)}) custom-call(s32[8]{0:T(128)} %group_ref.1, s32[2]{0:T(128)} %length_ref.1, s32[2]{0:T(128)} %pad_add_fusion.place_ref, s32[2,256]{1,0:T(2,128)} %table_ref.1, bf16[8,128,640]{2,1,0:T(8,128)(2,1)} %copy-done, bf16[8,128,640]{2,1,0:T(8,128)(2,1)} %copy-done.2, ...), custom_call_target="tpu_custom_call" | custom-call | tf_op jit(solution)/shard_map/attend/pallas_call | solution.py:299
  100.7 0.1 collective-permute-start.2
  100.9 3.2 %collective-permute-done.2.b_ref = bf16[8,136,640]{2,1,0:T(8,128)(2,1)S(1)} collective-permute-done((bf16[8,136,640]{2,1,0:T(8,128)(2,1)}, bf16[8,136,640]{2,1,0:T(8,128)(2,1)S(1)}, u32[]{:S(2)}, u32[]{:S(2)}) %collective-permute-start.2) | collective-permute-done | bytes 1392672 | tf_op jit(solution)/shard_map/ppermute | solution.py:333
  104.1 0.0 copy-start.1
  104.1 1.1 copy-done.1
  105.2 7.2 %pair.1 = bf16[8,136,640]{2,1,0:T(8,128)(2,1)} custom-call(bf16[8,136,640]{2,1,0:T(8,128)(2,1)} %get-tuple-element.15.a_ref, bf16[8,136,640]{2,1,0:T(8,128)(2,1)} %copy-done.1), custom_call_target="tpu_custom_call" | custom-call | tf_op jit(solution)/shard_map/pair/pallas_call | solution.py:334
  112.4 41.5 %all_to_all.16.in_ref = bf16[8,136,640]{2,1,0:T(8,128)(2,1)} all-to-all(bf16[8,136,640]{2,1,0:T(8,128)(2,1)} %pair.1), channel_id=1, replica_groups={{0,32,64,96,128,160,192,224},{8,40,72,104,136,168,200,232},{16,48,80,11..., dimensions={0} | all-to-all | bytes 2785280 | tf_op jit(solution)/shard_map/all_to_all | solution.py:342
  153.9 3.0 %many.1 = (bf16[1,72,640]{2,1,0:T(8,128)(2,1)}, bf16[1,72,640]{2,1,0:T(8,128)(2,1)}) custom-call(bf16[8,136,640]{2,1,0:T(8,128)(2,1)} %all_to_all.16.in_ref), custom_call_target="tpu_custom_call" | custom-call | tf_op jit(solution)/shard_map/many/pallas_call | solution.py:346
  156.9 0.7 collective-permute-start.3
  157.5 4.1 %collective-permute-done.3.b_ref = bf16[1,72,640]{2,1,0:T(8,128)(2,1)S(1)} collective-permute-done((bf16[1,72,640]{2,1,0:T(8,128)(2,1)}, bf16[1,72,640]{2,1,0:T(8,128)(2,1)S(1)}, u32[]{:S(2)}, u32[]{:S(2)}) %collective-permute-start.3) | collective-permute-done | bytes 92192 | tf_op jit(solution)/shard_map/ppermute | solution.py:349
  161.6 0.0 copy-start.4
  161.6 0.6 copy-done.4
  162.3 1.9 %last.1 = bf16[64,640]{1,0:T(8,128)(2,1)} custom-call(bf16[1,72,640]{2,1,0:T(8,128)(2,1)} %get-tuple-element.17.a_ref, bf16[1,72,640]{2,1,0:T(8,128)(2,1)} %copy-done.4), custom_call_target="tpu_custom_call" | custom-call | tf_op jit(solution)/shard_map/last/pallas_call | solution.py:350
Async XLA Ops:
  1.7 14.7 %all-to-all-start = ((f32[8,8,128]{2,1,0:T(8,128)}), f32[8,8,128]{2,1,0:T(8,128)S(1)}, u32[]{:S(2)}, u32[]{:S(2)}) async-start(f32[8,8,128]{2,1,0:T(8,128)} %sums.1), calls=%async_computation | async-start | bytes 65536 | tf_op jit(solution)/shard_map/all_to_all | solution.py:273
  16.4 0.6 copy-start.3
  18.9 4.7 %collective-permute-start = (bf16[64,640]{1,0:T(8,128)(2,1)}, bf16[64,640]{1,0:T(8,128)(2,1)S(1)}, u32[]{:S(2)}, u32[]{:S(2)}) collective-permute-start(bf16[64,640]{1,0:T(8,128)(2,1)} %get-tuple-element.12), channel_id=1, source_target_pairs={{0,16},{8,24},{16,0},{24,8},{32,48},{40,56},{48,32},{56,40},{64,80... | collective-permute-start | bytes 245768 | tf_op jit(solution)/shard_map/ppermute | solution.py:284
  61.6 3.0 %copy-start = (bf16[8,128,640]{2,1,0:T(8,128)(2,1)}, bf16[8,128,640]{2,1,0:T(8,128)(2,1)S(1)}, u32[]{:S(2)}) copy-start(bf16[8,128,640]{2,1,0:T(8,128)(2,1)S(1)} %all_to_all.15.qa_ref) | copy-start | bytes 3932164
  61.6 3.0 %collective-permute-start.1 = (bf16[8,128,640]{2,1,0:T(8,128)(2,1)S(1)}, bf16[8,128,640]{2,1,0:T(8,128)(2,1)S(1)}, u32[]{:S(2)}, u32[]{:S(2)}) collective-permute-start(bf16[8,128,640]{2,1,0:T(8,128)(2,1)S(1)} %all_to_all.15.qa_ref), channel_id=1, source_target_pairs={{0,8},{8,0},{16,24},{24,16},{32,40},{40,32},{48,56},{56,48},{64,72... | collective-permute-start | bytes 3932168 | tf_op jit(solution)/shard_map/ppermute | solution.py:291
  64.6 1.1 copy-start.2
  100.7 3.4 %collective-permute-start.2 = (bf16[8,136,640]{2,1,0:T(8,128)(2,1)}, bf16[8,136,640]{2,1,0:T(8,128)(2,1)S(1)}, u32[]{:S(2)}, u32[]{:S(2)}) collective-permute-start(bf16[8,136,640]{2,1,0:T(8,128)(2,1)} %get-tuple-element.16), channel_id=1, source_target_pairs={{0,8},{8,0},{16,24},{24,16},{32,40},{40,32},{48,56},{56,48},{64,72... | collective-permute-start | bytes 4177928 | tf_op jit(solution)/shard_map/ppermute | solution.py:333
  104.1 1.1 copy-start.1
  156.9 4.8 %collective-permute-start.3 = (bf16[1,72,640]{2,1,0:T(8,128)(2,1)}, bf16[1,72,640]{2,1,0:T(8,128)(2,1)S(1)}, u32[]{:S(2)}, u32[]{:S(2)}) collective-permute-start(bf16[1,72,640]{2,1,0:T(8,128)(2,1)} %get-tuple-element.18), channel_id=1, source_target_pairs={{0,16},{8,24},{16,0},{24,8},{32,48},{40,56},{48,32},{56,40},{64,80... | collective-permute-start | bytes 276488 | tf_op jit(solution)/shard_map/ppermute | solution.py:349
  161.6 0.6 copy-start.4

commit v2 on v1

v2 whole, which is shorter than its diff:
```python
import functools
import math

import jax
import jax.numpy as jnp
from jax import lax
from jax.experimental import pallas as pl
from jax.experimental.pallas import tpu as pltpu
from jax.sharding import PartitionSpec as P

HDIM = 128
GROUPS = 2
NEWTOK = 256
EPSILON = 1e-06
MASKED = -1e30
STAT_ROWS = 8
SPLITS = ((0, 2), (2, 2), (4, 1))


def pieces(values):
    high = values.astype(jnp.bfloat16)
    rest = values - high.astype(jnp.float32)
    middle = rest.astype(jnp.bfloat16)
    low = (rest - middle.astype(jnp.float32)).astype(jnp.bfloat16)
    return high, middle, low


def to_columns(rows):
    count = rows.shape[0]
    if count < 128:
        rows = jnp.concatenate([rows, jnp.zeros((128 - count, 128), jnp.float32)], axis=0)
    return rows.T


def sums_kernel(q_ref, k_ref, out_ref):
    tokens = q_ref.shape[0]
    query = q_ref[...].astype(jnp.float32)
    key = k_ref[...].astype(jnp.float32)
    query_sum = jnp.sum(query * query, axis=1, keepdims=True)
    key_sum = jnp.sum(key * key, axis=1, keepdims=True)
    lane = lax.broadcasted_iota(jnp.int32, (tokens, 128), 1)
    both = jnp.where(lane == 0, query_sum, jnp.where(lane == 1, key_sum, 0.0))
    padded = jnp.concatenate([both, jnp.zeros((128 - tokens, 128), jnp.float32)], axis=0)
    rows = padded.T[0:8]
    for index in range(out_ref.shape[0]):
        out_ref[index] = rows


def norm_kernel(
    q_ref, k_ref, v_ref, qg_ref, kg_ref, sums_ref, *outs, full_width, scale, splits
):
    tokens, width = q_ref.shape
    spread_refs, (k_out, v_out) = outs[: len(splits)], outs[len(splits) :]
    total = sums_ref[0]
    for index in range(1, sums_ref.shape[0]):
        total = total + sums_ref[index]
    inverse = to_columns(lax.rsqrt(total / full_width + EPSILON))
    query_inverse = inverse[0:tokens, 0:1]
    key_inverse = inverse[0:tokens, 1:2]
    queries = (
        q_ref[...].astype(jnp.float32) * query_inverse * (qg_ref[...] * scale)
    ).astype(jnp.bfloat16)
    for (first, count), spread_ref in zip(splits, spread_refs):
        part = queries[:, first * HDIM : (first + count) * HDIM]
        for index in range(spread_ref.shape[0]):
            spread_ref[index] = part
    k_out[0:tokens] = (
        k_ref[...].astype(jnp.float32) * key_inverse * kg_ref[...]
    ).astype(jnp.bfloat16)
    v_out[0:tokens] = v_ref[...]
    blank = jnp.zeros((k_out.shape[0] - tokens, width), jnp.bfloat16)
    k_out[tokens:] = blank
    v_out[tokens:] = blank


def read_lse(ref, index, rows):
    found = []
    for first in range(0, ref.shape[2], HDIM):
        block = ref[index, rows : rows + STAT_ROWS, first : first + HDIM].astype(jnp.float32)
        found.append(block[0:1] + block[1:2] + block[2:3])
    return jnp.concatenate(found, axis=0)


def write_lse(ref, index, rows, lse):
    row = lax.broadcasted_iota(jnp.int32, (STAT_ROWS, 128), 0)
    for head in range(lse.shape[0]):
        high, middle, low = (
            piece.astype(jnp.float32) for piece in pieces(lse[head : head + 1])
        )
        block = jnp.where(
            row == 0, high, jnp.where(row == 1, middle, jnp.where(row == 2, low, 0.0))
        )
        ref[index, rows : rows + STAT_ROWS, head * HDIM : (head + 1) * HDIM] = block.astype(
            jnp.bfloat16
        )


def attend_kernel(
    group_ref,
    length_ref,
    place_ref,
    table_ref,
    q00_ref,
    q01_ref,
    q10_ref,
    q11_ref,
    key_ref,
    value_ref,
    own_key_ref,
    own_value_ref,
    oa_ref,
    ob_ref,
    bias_ref,
    *,
    first,
    pages,
    page_len,
    tok_dev,
):
    request = pl.program_id(0)
    group = group_ref[request]
    seq_index = place_ref[0]
    own_request = place_ref[1]
    cached = pages * page_len
    own_rows = own_key_ref.shape[0]
    heads = oa_ref.shape[2] // HDIM
    rows = 2 * tok_dev

    @pl.when(request == 0)
    def _():
        lane = lax.broadcasted_iota(jnp.int32, (1, page_len), 1)
        page_ids = lax.broadcasted_iota(jnp.int32, (1, table_ref.shape[1]), 1)
        for group_id in range(GROUPS):
            table_row = table_ref[group_id : group_id + 1, :]
            for page in range(pages):
                slot = seq_index * (GROUPS * pages) + group_id * pages + page
                logical = jnp.sum(
                    jnp.where(table_row == slot, page_ids, 0), axis=1, keepdims=True
                )
                usable = logical * page_len + lane < length_ref[group_id]
                bias_ref[group_id, 0:1, page * page_len : (page + 1) * page_len] = jnp.where(
                    usable, 0.0, MASKED
                )

    def body(masked):
        if masked:
            own_lane = lax.broadcasted_iota(jnp.int32, (1, own_rows), 1)
            limit = jnp.where(request == own_request, tok_dev, 0)
            own_bias = jnp.where(own_lane < limit, 0.0, MASKED)
        lane = lax.broadcasted_iota(jnp.int32, (2 * rows, 128), 1)
        stats = jnp.zeros((2 * rows, 128), jnp.float32)
        for head in range(heads):
            here = slice(head * HDIM, (head + 1) * HDIM)
            there = slice((first + head) * HDIM, (first + head + 1) * HDIM)
            query = jnp.concatenate(
                [ref[0, :, here] for ref in (q00_ref, q01_ref, q10_ref, q11_ref)], axis=0
            )
            keys = key_ref[pl.ds(group * pages, pages), :, here].reshape(cached, HDIM)
            values = value_ref[pl.ds(group * pages, pages), :, here].reshape(cached, HDIM)
            scores = lax.dot_general(
                query, keys, (((1,), (1,)), ((), ())), preferred_element_type=jnp.float32
            )
            if masked:
                scores = scores + bias_ref[group]
                own_scores = lax.dot_general(
                    query,
                    own_key_ref[:, there],
                    (((1,), (1,)), ((), ())),
                    preferred_element_type=jnp.float32,
                )
                own_scores = own_scores + own_bias
            top = jnp.max(scores, axis=1, keepdims=True)
            if masked:
                top = jnp.maximum(top, jnp.max(own_scores, axis=1, keepdims=True))
            weights = jnp.exp2(scores - top)
            total = jnp.sum(weights, axis=1, keepdims=True)
            mixed = jnp.dot(
                weights.astype(jnp.bfloat16), values, preferred_element_type=jnp.float32
            )
            if masked:
                own_weights = jnp.exp2(own_scores - top)
                total = total + jnp.sum(own_weights, axis=1, keepdims=True)
                mixed = mixed + jnp.dot(
                    own_weights.astype(jnp.bfloat16),
                    own_value_ref[:, there],
                    preferred_element_type=jnp.float32,
                )
            mixed = (mixed * (1.0 / total)).astype(jnp.bfloat16)
            oa_ref[0, 0:rows, here] = mixed[0:rows]
            ob_ref[0, 0:rows, here] = mixed[rows:]
            stats = jnp.where(lane == head, top + jnp.log2(total), stats)
        write_lse(oa_ref, 0, rows, stats[0:rows].T[0:heads])
        write_lse(ob_ref, 0, rows, stats[rows:].T[0:heads])

    plain = (length_ref[group] == table_ref.shape[1] * page_len) & (request != own_request)

    @pl.when(plain)
    def _():
        body(False)

    @pl.when(jnp.logical_not(plain))
    def _():
        body(True)


def merge_weights(stats):
    top = functools.reduce(jnp.maximum, stats)
    weights = [jnp.exp2(stat - top) for stat in stats]
    total = functools.reduce(jnp.add, weights)
    return [weight / total for weight in weights], top + jnp.log2(total)


def pair_kernel(a_ref, b_ref, *out_refs):
    count = a_ref.shape[0]
    rows = a_ref.shape[1] - STAT_ROWS
    heads = a_ref.shape[2] // HDIM
    factors = []
    joint = []
    for index in range(count):
        weights, lse = merge_weights([read_lse(a_ref, index, rows), read_lse(b_ref, index, rows)])
        factors += weights
        joint.append(lse)
    columns = to_columns(jnp.concatenate(factors, axis=0))[0:rows]
    part = rows // len(out_refs)
    for index in range(count):
        for head in range(heads):
            lane = 2 * index * heads + head
            here = slice(head * HDIM, (head + 1) * HDIM)
            merged = (
                a_ref[index, 0:rows, here].astype(jnp.float32) * columns[:, lane : lane + 1]
                + b_ref[index, 0:rows, here].astype(jnp.float32)
                * columns[:, lane + heads : lane + heads + 1]
            ).astype(jnp.bfloat16)
            for place, out_ref in enumerate(out_refs):
                out_ref[index, 0:part, here] = merged[place * part : (place + 1) * part]
        for place, out_ref in enumerate(out_refs):
            lse = joint[index]
            if place:
                lse = jnp.concatenate([lse[:, part:], lse[:, 0:part]], axis=1)
            write_lse(out_ref, index, part, lse)


def final_kernel(in_ref, *refs):
    out_ref = refs[-1]
    done = 0
    for ref in refs[:-1]:
        out_ref[:, done : done + ref.shape[1]] = ref[...]
        done += ref.shape[1]
    count = in_ref.shape[0]
    rows = in_ref.shape[1] - STAT_ROWS
    heads = in_ref.shape[2] // HDIM
    weights, _ = merge_weights([read_lse(in_ref, index, rows) for index in range(count)])
    columns = to_columns(jnp.concatenate(weights, axis=0))[0:rows]
    for head in range(heads):
        here = slice(head * HDIM, (head + 1) * HDIM)
        merged = None
        for index in range(count):
            lane = index * heads + head
            term = in_ref[index, 0:rows, here].astype(jnp.float32) * columns[:, lane : lane + 1]
            merged = term if merged is None else merged + term
        out_ref[:, done + head * HDIM : done + (head + 1) * HDIM] = merged.astype(jnp.bfloat16)


def merge_pairs(one, two, parts, step, name):
    count, size, width = one.shape
    rows = (size - STAT_ROWS) // parts + STAT_ROWS
    shape = jax.ShapeDtypeStruct((count, rows, width), jnp.bfloat16)
    out = pl.pallas_call(
        pair_kernel,
        out_shape=(shape,) * parts,
        grid=(count // step,),
        in_specs=[pl.BlockSpec((step, size, width), lambda r: (r, 0, 0))] * 2,
        out_specs=(pl.BlockSpec((step, rows, width), lambda r: (r, 0, 0)),) * parts,
        name=name,
    )(one, two)
    return out


def on_device(
    q_raw,
    k_raw,
    v_new,
    q_gain,
    k_gain,
    cache_keys,
    cache_values,
    page_table,
    cached_lengths,
    req_group,
):
    tok_dev, width = q_raw.shape
    tp_count = lax.axis_size("tp")
    seq_count = lax.axis_size("seq")
    heads = width // HDIM
    page_len = cache_keys.shape[1]
    pages = cache_keys.shape[0] // GROUPS
    requests = req_group.shape[0]
    plane = seq_count // requests
    seq_index = lax.axis_index("seq")
    bf16 = jnp.bfloat16
    f32 = jnp.float32
    scale = math.log2(math.e) / math.sqrt(HDIM)
    z_groups = [[z * plane + member for z in range(requests)] for member in range(plane)]
    core_pairs = [(index, index ^ 1) for index in range(seq_count)]
    y_pairs = [(index, index ^ 2) for index in range(seq_count)]
    splits = SPLITS

    def z_exchange(array):
        return lax.all_to_all(
            array, "seq", split_axis=0, concat_axis=0, tiled=True, axis_index_groups=z_groups
        )

    sums = pl.pallas_call(
        sums_kernel, out_shape=jax.ShapeDtypeStruct((tp_count, 8, 128), f32), name="sums"
    )(q_raw, k_raw)
    sums = lax.all_to_all(sums, "tp", split_axis=0, concat_axis=0, tiled=True)
    *spread, own_keys, own_values = pl.pallas_call(
        functools.partial(
            norm_kernel, full_width=float(width * tp_count), scale=scale, splits=splits
        ),
        out_shape=tuple(
            jax.ShapeDtypeStruct((requests, tok_dev, count * HDIM), bf16) for _, count in splits
        )
        + (jax.ShapeDtypeStruct((128, width), bf16),) * 2,
        name="norm",
    )(q_raw, k_raw, v_new, q_gain[None, :], k_gain[None, :], sums)

    place = jnp.stack([seq_index, seq_index // plane]).astype(jnp.int32)
    rows = 2 * tok_dev
    chunk = rows + STAT_ROWS

    def attend(first, count, queries):
        part = count * HDIM
        block_q = pl.BlockSpec((1, tok_dev, part), lambda r, *_: (r, 0, 0))
        block_o = pl.BlockSpec((1, chunk, part), lambda r, *_: (r, 0, 0))
        block_kv = pl.BlockSpec(
            (pl.Element(GROUPS * pages), pl.Element(page_len), pl.Element(part)), lambda r, *_: (0, 0, first * HDIM)
        )
        whole = lambda array: pl.BlockSpec(array.shape, lambda r, *_: (0,) * array.ndim)
        shape = jax.ShapeDtypeStruct((requests, chunk, part), bf16)
        return pl.pallas_call(
            functools.partial(
                attend_kernel, first=first, pages=pages, page_len=page_len, tok_dev=tok_dev
            ),
            out_shape=(shape, shape),
            grid_spec=pltpu.PrefetchScalarGridSpec(
                num_scalar_prefetch=3,
                grid=(requests,),
                in_specs=[whole(page_table)]
                + [block_q] * 4
                + [block_kv, block_kv, whole(own_keys), whole(own_values)],
                out_specs=(block_o, block_o),
                scratch_shapes=[pltpu.VMEM((GROUPS, 1, pages * page_len), f32)],
            ),
            name="attend",
        )(
            req_group,
            cached_lengths,
            place,
            page_table,
            *queries,
            cache_keys,
            cache_values,
            own_keys,
            own_values,
        )

    finished = []
    for (first, count), array in zip(splits, spread):
        q00 = z_exchange(array)
        q01 = lax.ppermute(q00, "seq", y_pairs)
        q10 = lax.ppermute(q00, "seq", core_pairs)
        q11 = lax.ppermute(q01, "seq", core_pairs)
        out_a, out_b = attend(first, count, (q00, q01, q10, q11))
        out_b = lax.ppermute(out_b, "seq", core_pairs)
        keep, send = merge_pairs(out_a, out_b, 2, requests // 2, "cores")
        send = lax.ppermute(send, "seq", y_pairs)
        (merged,) = merge_pairs(keep, send, 1, requests // 2, "sides")
        merged = z_exchange(merged)
        last = first + count == heads
        finished.append(
            pl.pallas_call(
                final_kernel,
                out_shape=jax.ShapeDtypeStruct(
                    (tok_dev, width if last else count * HDIM), bf16
                ),
                name="final",
            )(merged, *(finished if last else ()))
        )
    return finished[-1]


def solution(mesh):
    return jax.shard_map(
        on_device,
        mesh=mesh,
        in_specs=(
            P("seq", "tp"),
            P("seq", "tp"),
            P("seq", "tp"),
            P("tp"),
            P("tp"),
            P("seq", None, "tp"),
            P("seq", None, "tp"),
            P(),
            P(),
            P(),
        ),
        out_specs=P("seq", "tp"),
        check_vma=False,
    )
```

time: 167 us -> 175 us (1.048)
  the two profiles are of different devices: /device:TPU:64 before, /device:TPU:8 now
where the time goes in v2:
time: 175 us; the launch traced here: 173 us
  Pallas kernels  60.9 us (35%)
  waiting for transfers between devices  43.2 us (25%)
  starting transfers between devices  38.1 us (22%)
  blocking collectives  18.9 us (11%)
  local copies, waits for them, and re-layouts  11.4 us (7%)
    pallas_call x3, Pallas kernels, attend(): pl.pallas_call(functools.partial(attend_kernel, first=first, pages=pages,...  36.4 us
    all_to_all x5, starting transfers between devices, z_exchange(): lax.all_to_all(array, 'seq', split_axis=0, concat_axis=0, tiled=True, axi...  24.2 us
    all_to_all x1, blocking collectives, z_exchange(): lax.all_to_all(array, 'seq', split_axis=0, concat_axis=0, tiled=True, axi...  18.9 us
    pallas_call x6, Pallas kernels, merge_pairs(): pl.pallas_call(pair_kernel, out_shape=(shape,) * parts, grid=(count // st...  14.9 us
    ppermute x3, waiting for transfers between devices, on_device(): q01 = lax.ppermute(q00, 'seq', y_pairs)  13.6 us
    all_to_all x5, waiting for transfers between devices, z_exchange(): lax.all_to_all(array, 'seq', split_axis=0, concat_axis=0, tiled=True, axi...  10.3 us
    ppermute x3, waiting for transfers between devices, on_device(): send = lax.ppermute(send, 'seq', y_pairs)  10.3 us
    unnamed x44, local copies, waits for them, and re-layouts  8.84 us
  transfers between devices with their start and end apart: 21, of which 11 were waited for; matrix products, arithmetic and copies ran while one was open for 2% of the time, Pallas kernels for 32%

profile of v2, /device:TPU:8, one launch (start us, length us, event | category | flops | bytes accessed | tf_op | source)
XLA Modules:
  0.0 173.4 jit_solution(14776877434091982978)
XLA Ops:
  0.0 1.7 sums.1
  1.7 6.0 %all-to-all-start = ((f32[8,8,128]{2,1,0:T(8,128)}), f32[8,8,128]{2,1,0:T(8,128)S(1)}, u32[]{:S(2)}, u32[]{:S(2)}) async-start(f32[8,8,128]{2,1,0:T(8,128)} %sums.1), calls=%async_computation | async-start | bytes 65536 | tf_op jit(solution)/shard_map/all_to_all | solution.py:316
  7.7 1.3 broadcast_in_dim.6.qg_ref
  9.0 1.3 broadcast_in_dim.7.kg_ref
  10.3 5.2 %all-to-all-done.sums_ref = f32[8,8,128]{2,1,0:T(8,128)S(1)} async-done(((f32[8,8,128]{2,1,0:T(8,128)}), f32[8,8,128]{2,1,0:T(8,128)S(1)}, u32[]{:S(2)}, u32[]{:S(2)}) %all-to-all-start) | async-done | bytes 32800 | tf_op jit(solution)/shard_map/all_to_all | solution.py:316
  16.1 2.1 %norm.1 = (bf16[8,64,256]{2,1,0:T(8,128)(2,1)}, bf16[8,64,256]{2,1,0:T(8,128)(2,1)}, bf16[8,64,128]{2,1,0:T(8,128)(2,1)}, bf16[128,640]{1,0:T(8,128)(2,1)}, bf16[128,640]{1,0:T(8,128)(2,1)}) custom-call(bf16[64,640]{1,0:T(8,128)(2,1)} %q_ref.3, bf16[64,640]{1,0:T(8,128)(2,1)} %k_ref.3, bf16[64,640]{1,0:T(8,128)(2,1)} %v_ref.1, ...), custom_call_target="tpu_custom_call" | custom-call | tf_op jit(solution)/shard_map/norm/pallas_call | solution.py:317
  18.2 18.9 %all_to_all.35.q00_ref = bf16[8,64,256]{2,1,0:T(8,128)(2,1)S(1)} all-to-all(bf16[8,64,256]{2,1,0:T(8,128)(2,1)} %get-tuple-element.34), channel_id=1, replica_groups={{0,32,64,96,128,160,192,224},{8,40,72,104,136,168,200,232},{16,48,80,11..., dimensions={0} | all-to-all | bytes 524288 | tf_op jit(solution)/shard_map/all_to_all | solution.py:309
  37.2 3.4 %all-to-all-start.3 = ((bf16[8,64,256]{2,1,0:T(8,128)(2,1)}), bf16[8,64,256]{2,1,0:T(8,128)(2,1)S(1)}, u32[]{:S(2)}, u32[]{:S(2)}) async-start(bf16[8,64,256]{2,1,0:T(8,128)(2,1)} %get-tuple-element.29), calls=%async_computation.3 | async-start | bytes 524288 | tf_op jit(solution)/shard_map/all_to_all | solution.py:309
  40.6 1.4 collective-permute-start.10
  42.0 5.0 %collective-permute-done.10.q01_ref = bf16[8,64,256]{2,1,0:T(8,128)(2,1)S(1)} collective-permute-done((bf16[8,64,256]{2,1,0:T(8,128)(2,1)S(1)}, bf16[8,64,256]{2,1,0:T(8,128)(2,1)S(1)}, u32[]{:S(2)}, u32[]{:S(2)}) %collective-permute-start.10) | collective-permute-done | bytes 262176 | tf_op jit(solution)/shard_map/ppermute | solution.py:371
  47.1 3.9 %all-to-all-done.3.q00_ref = bf16[8,64,256]{2,1,0:T(8,128)(2,1)S(1)} async-done(((bf16[8,64,256]{2,1,0:T(8,128)(2,1)}), bf16[8,64,256]{2,1,0:T(8,128)(2,1)S(1)}, u32[]{:S(2)}, u32[]{:S(2)}) %all-to-all-start.3) | async-done | bytes 262176 | tf_op jit(solution)/shard_map/all_to_all | solution.py:309
  51.0 1.3 collective-permute-start.5
  53.0 0.7 copy-done.12
  53.8 13.6 %attend.5 = (bf16[8,136,256]{2,1,0:T(8,128)(2,1)}, bf16[8,136,256]{2,1,0:T(8,128)(2,1)}) custom-call(s32[8]{0:T(128)} %group_ref.5, s32[2]{0:T(128)} %length_ref.5, s32[2]{0:T(128)} %pad_add_fusion.place_ref, s32[2,256]{1,0:T(2,128)} %table_ref.5, bf16[8,64,256]{2,1,0:T(8,128)(2,1)} %copy-done.3, bf16[8,64,256]{2,1,0:T(8,128)(2,1)} %copy-done.11, ...), custom_call_target="tpu_custom_call" | custom-call | tf_op jit(solution)/shard_map/attend/pallas_call | solution.py:341
  68.0 1.9 %collective-permute-done.6.q10_ref = bf16[8,64,256]{2,1,0:T(8,128)(2,1)S(1)} collective-permute-done((bf16[8,64,256]{2,1,0:T(8,128)(2,1)S(1)}, bf16[8,64,256]{2,1,0:T(8,128)(2,1)S(1)}, u32[]{:S(2)}, u32[]{:S(2)}) %collective-permute-start.6) | collective-permute-done | bytes 262176 | tf_op jit(solution)/shard_map/ppermute | solution.py:372
  70.6 0.7 copy-done.16
  71.3 13.6 %attend.4 = (bf16[8,136,256]{2,1,0:T(8,128)(2,1)}, bf16[8,136,256]{2,1,0:T(8,128)(2,1)}) custom-call(s32[8]{0:T(128)} %group_ref.5, s32[2]{0:T(128)} %length_ref.5, s32[2]{0:T(128)} %pad_add_fusion.place_ref, s32[2,256]{1,0:T(2,128)} %table_ref.5, bf16[8,64,256]{2,1,0:T(8,128)(2,1)} %copy-done.2, bf16[8,64,256]{2,1,0:T(8,128)(2,1)} %copy-done.14, ...), custom_call_target="tpu_custom_call" | custom-call | tf_op jit(solution)/shard_map/attend/pallas_call | solution.py:341
  85.1 0.8 copy-done.6
  85.9 2.8 %cores.5 = (bf16[8,72,256]{2,1,0:T(8,128)(2,1)}, bf16[8,72,256]{2,1,0:T(8,128)(2,1)}) custom-call(bf16[8,136,256]{2,1,0:T(8,128)(2,1)} %get-tuple-element.35.a_ref, bf16[8,136,256]{2,1,0:T(8,128)(2,1)} %copy-done.6), custom_call_target="tpu_custom_call" | custom-call | tf_op jit(solution)/shard_map/cores/pallas_call | solution.py:268
  88.8 0.7 collective-permute-start.14
  89.4 3.4 %all-to-all-start.1 = ((bf16[8,64,128]{2,1,0:T(8,128)(2,1)}), bf16[8,64,128]{2,1,0:T(8,128)(2,1)S(1)}, u32[]{:S(2)}, u32[]{:S(2)}) async-start(bf16[8,64,128]{2,1,0:T(8,128)(2,1)} %get-tuple-element.22), calls=%async_computation.1 | async-start | bytes 262144 | tf_op jit(solution)/shard_map/all_to_all | solution.py:309
  92.8 5.4 %collective-permute-done.14.b_ref = bf16[8,72,256]{2,1,0:T(8,128)(2,1)S(1)} collective-permute-done((bf16[8,72,256]{2,1,0:T(8,128)(2,1)}, bf16[8,72,256]{2,1,0:T(8,128)(2,1)S(1)}, u32[]{:S(2)}, u32[]{:S(2)}) %collective-permute-start.14) | collective-permute-done | bytes 294944 | tf_op jit(solution)/shard_map/ppermute | solution.py:377
  98.3 0.7 copy-done.9
  99.0 2.4 %sides.5 = bf16[8,72,256]{2,1,0:T(8,128)(2,1)} custom-call(bf16[8,72,256]{2,1,0:T(8,128)(2,1)} %get-tuple-element.37.a_ref, bf16[8,72,256]{2,1,0:T(8,128)(2,1)} %copy-done.9), custom_call_target="tpu_custom_call" | custom-call | tf_op jit(solution)/shard_map/sides/pallas_call | solution.py:268
  101.3 1.0 all-to-all-done.1.q00_ref
  102.3 3.4 %all-to-all-start.6 = ((bf16[8,72,256]{2,1,0:T(8,128)(2,1)}), bf16[8,72,256]{2,1,0:T(8,128)(2,1)S(1)}, u32[]{:S(2)}, u32[]{:S(2)}) async-start(bf16[8,72,256]{2,1,0:T(8,128)(2,1)} %sides.5), calls=%async_computation.6 | async-start | bytes 589824 | tf_op jit(solution)/shard_map/all_to_all | solution.py:309
  105.8 0.8 copy-done.5
  106.6 2.8 %cores.4 = (bf16[8,72,256]{2,1,0:T(8,128)(2,1)}, bf16[8,72,256]{2,1,0:T(8,128)(2,1)}) custom-call(bf16[8,136,256]{2,1,0:T(8,128)(2,1)} %get-tuple-element.30.a_ref, bf16[8,136,256]{2,1,0:T(8,128)(2,1)} %copy-done.5), custom_call_target="tpu_custom_call" | custom-call | tf_op jit(solution)/shard_map/cores/pallas_call | solution.py:268
  109.4 1.3 collective-permute-start.9
  110.8 0.7 collective-permute-start
  111.4 8.6 %collective-permute-done.q01_ref = bf16[8,64,128]{2,1,0:T(8,128)(2,1)S(1)} collective-permute-done((bf16[8,64,128]{2,1,0:T(8,128)(2,1)S(1)}, bf16[8,64,128]{2,1,0:T(8,128)(2,1)S(1)}, u32[]{:S(2)}, u32[]{:S(2)}) %collective-permute-start) | collective-permute-done | bytes 131104 | tf_op jit(solution)/shard_map/ppermute | solution.py:371
  120.1 0.7 copy-done.8
  120.8 2.4 %sides.4 = bf16[8,72,256]{2,1,0:T(8,128)(2,1)} custom-call(bf16[8,72,256]{2,1,0:T(8,128)(2,1)} %get-tuple-element.32.a_ref, bf16[8,72,256]{2,1,0:T(8,128)(2,1)} %copy-done.8), custom_call_target="tpu_custom_call" | custom-call | tf_op jit(solution)/shard_map/sides/pallas_call | solution.py:268
  123.2 6.8 %all-to-all-start.4 = ((bf16[8,72,256]{2,1,0:T(8,128)(2,1)}), bf16[8,72,256]{2,1,0:T(8,128)(2,1)S(1)}, u32[]{:S(2)}, u32[]{:S(2)}) async-start(bf16[8,72,256]{2,1,0:T(8,128)(2,1)} %sides.4), calls=%async_computation.4 | async-start | bytes 589824 | tf_op jit(solution)/shard_map/all_to_all | solution.py:309
  131.3 9.2 %attend.3 = (bf16[8,136,128]{2,1,0:T(8,128)(2,1)}, bf16[8,136,128]{2,1,0:T(8,128)(2,1)}) custom-call(s32[8]{0:T(128)} %group_ref.5, s32[2]{0:T(128)} %length_ref.5, s32[2]{0:T(128)} %pad_add_fusion.place_ref, s32[2,256]{1,0:T(2,128)} %table_ref.5, bf16[8,64,128]{2,1,0:T(8,128)(2,1)} %copy-done.7, bf16[8,64,128]{2,1,0:T(8,128)(2,1)} %copy-done.18, ...), custom_call_target="tpu_custom_call" | custom-call | tf_op jit(solution)/shard_map/attend/pallas_call | solution.py:341
  140.8 1.6 collective-permute-done.3.b_ref
  142.4 0.7 copy-done.10
  143.1 2.4 %cores.3 = (bf16[8,72,128]{2,1,0:T(8,128)(2,1)}, bf16[8,72,128]{2,1,0:T(8,128)(2,1)}) custom-call(bf16[8,136,128]{2,1,0:T(8,128)(2,1)} %get-tuple-element.25.a_ref, bf16[8,136,128]{2,1,0:T(8,128)(2,1)} %copy-done.10), custom_call_target="tpu_custom_call" | custom-call | tf_op jit(solution)/shard_map/cores/pallas_call | solution.py:268
  145.5 1.3 collective-permute-start.4
  146.8 4.8 %collective-permute-done.4.b_ref = bf16[8,72,128]{2,1,0:T(8,128)(2,1)S(1)} collective-permute-done((bf16[8,72,128]{2,1,0:T(8,128)(2,1)}, bf16[8,72,128]{2,1,0:T(8,128)(2,1)S(1)}, u32[]{:S(2)}, u32[]{:S(2)}) %collective-permute-start.4) | collective-permute-done | bytes 147488 | tf_op jit(solution)/shard_map/ppermute | solution.py:377
  151.7 0.7 copy-done.17
  152.3 2.1 %sides.3 = bf16[8,72,128]{2,1,0:T(8,128)(2,1)} custom-call(bf16[8,72,128]{2,1,0:T(8,128)(2,1)} %get-tuple-element.27.a_ref, bf16[8,72,128]{2,1,0:T(8,128)(2,1)} %copy-done.17), custom_call_target="tpu_custom_call" | custom-call | tf_op jit(solution)/shard_map/sides/pallas_call | solution.py:268
  154.4 7.2 %all-to-all-start.2 = ((bf16[8,72,128]{2,1,0:T(8,128)(2,1)}), bf16[8,72,128]{2,1,0:T(8,128)(2,1)S(1)}, u32[]{:S(2)}, u32[]{:S(2)}) async-start(bf16[8,72,128]{2,1,0:T(8,128)(2,1)} %sides.3), calls=%async_computation.2 | async-start | bytes 294912 | tf_op jit(solution)/shard_map/all_to_all | solution.py:309
  161.6 1.9 %final.4.refs_1_ = bf16[64,256]{1,0:T(8,128)(2,1)} custom-call(bf16[8,72,256]{2,1,0:T(8,128)(2,1)} %copy-done), custom_call_target="tpu_custom_call" | custom-call | tf_op jit(solution)/shard_map/final/pallas_call | solution.py:382
  163.5 1.9 %final.3.refs_0_ = bf16[64,256]{1,0:T(8,128)(2,1)} custom-call(bf16[8,72,256]{2,1,0:T(8,128)(2,1)} %copy-done.1), custom_call_target="tpu_custom_call" | custom-call | tf_op jit(solution)/shard_map/final/pallas_call | solution.py:382
  165.5 5.4 %all-to-all-done.2.in_ref = bf16[8,72,128]{2,1,0:T(8,128)(2,1)S(1)} async-done(((bf16[8,72,128]{2,1,0:T(8,128)(2,1)}), bf16[8,72,128]{2,1,0:T(8,128)(2,1)S(1)}, u32[]{:S(2)}, u32[]{:S(2)}) %all-to-all-start.2) | async-done | bytes 147488 | tf_op jit(solution)/shard_map/all_to_all | solution.py:309
  170.8 0.7 copy-done.4
  171.5 1.9 %final.5 = bf16[64,640]{1,0:T(8,128)(2,1)} custom-call(bf16[8,72,128]{2,1,0:T(8,128)(2,1)} %copy-done.4, bf16[64,256]{1,0:T(8,128)(2,1)} %final.3.refs_0_, bf16[64,256]{1,0:T(8,128)(2,1)} %final.4.refs_1_), custom_call_target="tpu_custom_call" | custom-call | tf_op jit(solution)/shard_map/final/pallas_call | solution.py:382
  (56 shorter events, 4.4 us)
Async XLA Ops:
  1.7 13.8 %all-to-all-start = ((f32[8,8,128]{2,1,0:T(8,128)}), f32[8,8,128]{2,1,0:T(8,128)S(1)}, u32[]{:S(2)}, u32[]{:S(2)}) async-start(f32[8,8,128]{2,1,0:T(8,128)} %sums.1), calls=%async_computation | async-start | bytes 65536 | tf_op jit(solution)/shard_map/all_to_all | solution.py:316
  15.5 0.6 copy-start.21
  37.2 15.8 %copy-start.3 = (bf16[8,64,256]{2,1,0:T(8,128)(2,1)}, bf16[8,64,256]{2,1,0:T(8,128)(2,1)S(1)}, u32[]{:S(2)}) copy-start(bf16[8,64,256]{2,1,0:T(8,128)(2,1)S(1)} %all_to_all.35.q00_ref) | copy-start | bytes 786436
  37.2 13.8 %all-to-all-start.3 = ((bf16[8,64,256]{2,1,0:T(8,128)(2,1)}), bf16[8,64,256]{2,1,0:T(8,128)(2,1)S(1)}, u32[]{:S(2)}, u32[]{:S(2)}) async-start(bf16[8,64,256]{2,1,0:T(8,128)(2,1)} %get-tuple-element.29), calls=%async_computation.3 | async-start | bytes 524288 | tf_op jit(solution)/shard_map/all_to_all | solution.py:309
  40.6 6.5 %collective-permute-start.10 = (bf16[8,64,256]{2,1,0:T(8,128)(2,1)S(1)}, bf16[8,64,256]{2,1,0:T(8,128)(2,1)S(1)}, u32[]{:S(2)}, u32[]{:S(2)}) collective-permute-start(bf16[8,64,256]{2,1,0:T(8,128)(2,1)S(1)} %all_to_all.35.q00_ref), channel_id=1, source_target_pairs={{0,16},{8,24},{16,0},{24,8},{32,48},{40,56},{48,32},{56,40},{64,80... | collective-permute-start | bytes 786440 | tf_op jit(solution)/shard_map/ppermute | solution.py:371
  42.0 11.0 %collective-permute-start.11 = (bf16[8,64,256]{2,1,0:T(8,128)(2,1)S(1)}, bf16[8,64,256]{2,1,0:T(8,128)(2,1)S(1)}, u32[]{:S(2)}, u32[]{:S(2)}) collective-permute-start(bf16[8,64,256]{2,1,0:T(8,128)(2,1)S(1)} %all_to_all.35.q00_ref), channel_id=1, source_target_pairs={{0,8},{8,0},{16,24},{24,16},{32,40},{40,32},{48,56},{56,48},{64,72... | collective-permute-start | bytes 786440 | tf_op jit(solution)/shard_map/ppermute | solution.py:372
  47.0 6.0 %copy-start.11 = (bf16[8,64,256]{2,1,0:T(8,128)(2,1)}, bf16[8,64,256]{2,1,0:T(8,128)(2,1)S(1)}, u32[]{:S(2)}) copy-start(bf16[8,64,256]{2,1,0:T(8,128)(2,1)S(1)} %collective-permute-done.10.q01_ref) | copy-start | bytes 786436
  47.0 5.9 %collective-permute-start.12 = (bf16[8,64,256]{2,1,0:T(8,128)(2,1)S(1)}, bf16[8,64,256]{2,1,0:T(8,128)(2,1)S(1)}, u32[]{:S(2)}, u32[]{:S(2)}) collective-permute-start(bf16[8,64,256]{2,1,0:T(8,128)(2,1)S(1)} %collective-permute-done.10.q01_ref), channel_id=1, source_target_pairs={{0,8},{8,0},{16,24},{24,16},{32,40},{40,32},{48,56},{56,48},{64,72... | collective-permute-start | bytes 786440 | tf_op jit(solution)/shard_map/ppermute | solution.py:373
  51.0 16.4 %copy-start.2 = (bf16[8,64,256]{2,1,0:T(8,128)(2,1)}, bf16[8,64,256]{2,1,0:T(8,128)(2,1)S(1)}, u32[]{:S(2)}) copy-start(bf16[8,64,256]{2,1,0:T(8,128)(2,1)S(1)} %all-to-all-done.3.q00_ref) | copy-start | bytes 786436
  51.0 16.9 %collective-permute-start.5 = (bf16[8,64,256]{2,1,0:T(8,128)(2,1)S(1)}, bf16[8,64,256]{2,1,0:T(8,128)(2,1)S(1)}, u32[]{:S(2)}, u32[]{:S(2)}) collective-permute-start(bf16[8,64,256]{2,1,0:T(8,128)(2,1)S(1)} %all-to-all-done.3.q00_ref), channel_id=1, source_target_pairs={{0,16},{8,24},{16,0},{24,8},{32,48},{40,56},{48,32},{56,40},{64,80... | collective-permute-start | bytes 786440 | tf_op jit(solution)/shard_map/ppermute | solution.py:371
  53.0 0.7 copy-start.12
  53.0 0.8 copy-start.13
  67.4 17.7 %collective-permute-start.13 = (bf16[8,136,256]{2,1,0:T(8,128)(2,1)}, bf16[8,136,256]{2,1,0:T(8,128)(2,1)S(1)}, u32[]{:S(2)}, u32[]{:S(2)}) collective-permute-start(bf16[8,136,256]{2,1,0:T(8,128)(2,1)} %get-tuple-element.36), channel_id=1, source_target_pairs={{0,8},{8,0},{16,24},{24,16},{32,40},{40,32},{48,56},{56,48},{64,72... | collective-permute-start | bytes 1671176 | tf_op jit(solution)/shard_map/ppermute | solution.py:375
  67.4 2.5 %collective-permute-start.6 = (bf16[8,64,256]{2,1,0:T(8,128)(2,1)S(1)}, bf16[8,64,256]{2,1,0:T(8,128)(2,1)S(1)}, u32[]{:S(2)}, u32[]{:S(2)}) collective-permute-start(bf16[8,64,256]{2,1,0:T(8,128)(2,1)S(1)} %all-to-all-done.3.q00_ref), channel_id=1, source_target_pairs={{0,8},{8,0},{16,24},{24,16},{32,40},{40,32},{48,56},{56,48},{64,72... | collective-permute-start | bytes 786440 | tf_op jit(solution)/shard_map/ppermute | solution.py:372
  67.9 2.4 %copy-start.14 = (bf16[8,64,256]{2,1,0:T(8,128)(2,1)}, bf16[8,64,256]{2,1,0:T(8,128)(2,1)S(1)}, u32[]{:S(2)}) copy-start(bf16[8,64,256]{2,1,0:T(8,128)(2,1)S(1)} %collective-permute-done.5.q01_ref) | copy-start | bytes 786436
  67.9 2.4 %collective-permute-start.7 = (bf16[8,64,256]{2,1,0:T(8,128)(2,1)S(1)}, bf16[8,64,256]{2,1,0:T(8,128)(2,1)S(1)}, u32[]{:S(2)}, u32[]{:S(2)}) collective-permute-start(bf16[8,64,256]{2,1,0:T(8,128)(2,1)S(1)} %collective-permute-done.5.q01_ref), channel_id=1, source_target_pairs={{0,8},{8,0},{16,24},{24,16},{32,40},{40,32},{48,56},{56,48},{64,72... | collective-permute-start | bytes 786440 | tf_op jit(solution)/shard_map/ppermute | solution.py:373
  69.9 0.7 copy-start.15
  70.6 0.7 copy-start.16
  85.0 20.8 %collective-permute-start.8 = (bf16[8,136,256]{2,1,0:T(8,128)(2,1)}, bf16[8,136,256]{2,1,0:T(8,128)(2,1)S(1)}, u32[]{:S(2)}, u32[]{:S(2)}) collective-permute-start(bf16[8,136,256]{2,1,0:T(8,128)(2,1)} %get-tuple-element.31), channel_id=1, source_target_pairs={{0,8},{8,0},{16,24},{24,16},{32,40},{40,32},{48,56},{56,48},{64,72... | collective-permute-start | bytes 1671176 | tf_op jit(solution)/shard_map/ppermute | solution.py:375
  85.1 0.8 copy-start.6
  88.8 9.5 %collective-permute-start.14 = (bf16[8,72,256]{2,1,0:T(8,128)(2,1)}, bf16[8,72,256]{2,1,0:T(8,128)(2,1)S(1)}, u32[]{:S(2)}, u32[]{:S(2)}) collective-permute-start(bf16[8,72,256]{2,1,0:T(8,128)(2,1)} %get-tuple-element.38), channel_id=1, source_target_pairs={{0,16},{8,24},{16,0},{24,8},{32,48},{40,56},{48,32},{56,40},{64,80... | collective-permute-start | bytes 884744 | tf_op jit(solution)/shard_map/ppermute | solution.py:377
  89.4 12.9 %all-to-all-start.1 = ((bf16[8,64,128]{2,1,0:T(8,128)(2,1)}), bf16[8,64,128]{2,1,0:T(8,128)(2,1)S(1)}, u32[]{:S(2)}, u32[]{:S(2)}) async-start(bf16[8,64,128]{2,1,0:T(8,128)(2,1)} %get-tuple-element.22), calls=%async_computation.1 | async-start | bytes 262144 | tf_op jit(solution)/shard_map/all_to_all | solution.py:309
  98.3 0.7 copy-start.9
  102.3 27.7 %copy-start.7 = (bf16[8,64,128]{2,1,0:T(8,128)(2,1)}, bf16[8,64,128]{2,1,0:T(8,128)(2,1)S(1)}, u32[]{:S(2)}) copy-start(bf16[8,64,128]{2,1,0:T(8,128)(2,1)S(1)} %all-to-all-done.1.q00_ref) | copy-start | bytes 393220
  102.3 20.9 %all-to-all-start.6 = ((bf16[8,72,256]{2,1,0:T(8,128)(2,1)}), bf16[8,72,256]{2,1,0:T(8,128)(2,1)S(1)}, u32[]{:S(2)}, u32[]{:S(2)}) async-start(bf16[8,72,256]{2,1,0:T(8,128)(2,1)} %sides.5), calls=%async_computation.6 | async-start | bytes 589824 | tf_op jit(solution)/shard_map/all_to_all | solution.py:309
  105.8 0.8 copy-start.5
  109.4 10.6 %collective-permute-start.9 = (bf16[8,72,256]{2,1,0:T(8,128)(2,1)}, bf16[8,72,256]{2,1,0:T(8,128)(2,1)S(1)}, u32[]{:S(2)}, u32[]{:S(2)}) collective-permute-start(bf16[8,72,256]{2,1,0:T(8,128)(2,1)} %get-tuple-element.33), channel_id=1, source_target_pairs={{0,16},{8,24},{16,0},{24,8},{32,48},{40,56},{48,32},{56,40},{64,80... | collective-permute-start | bytes 884744 | tf_op jit(solution)/shard_map/ppermute | solution.py:377
  110.8 9.3 %collective-permute-start = (bf16[8,64,128]{2,1,0:T(8,128)(2,1)S(1)}, bf16[8,64,128]{2,1,0:T(8,128)(2,1)S(1)}, u32[]{:S(2)}, u32[]{:S(2)}) collective-permute-start(bf16[8,64,128]{2,1,0:T(8,128)(2,1)S(1)} %all-to-all-done.1.q00_ref), channel_id=1, source_target_pairs={{0,16},{8,24},{16,0},{24,8},{32,48},{40,56},{48,32},{56,40},{64,80... | collective-permute-start | bytes 393224 | tf_op jit(solution)/shard_map/ppermute | solution.py:371
  111.4 18.6 %collective-permute-start.1 = (bf16[8,64,128]{2,1,0:T(8,128)(2,1)S(1)}, bf16[8,64,128]{2,1,0:T(8,128)(2,1)S(1)}, u32[]{:S(2)}, u32[]{:S(2)}) collective-permute-start(bf16[8,64,128]{2,1,0:T(8,128)(2,1)S(1)} %all-to-all-done.1.q00_ref), channel_id=1, source_target_pairs={{0,8},{8,0},{16,24},{24,16},{32,40},{40,32},{48,56},{56,48},{64,72... | collective-permute-start | bytes 393224 | tf_op jit(solution)/shard_map/ppermute | solution.py:372
  120.0 10.0 %copy-start.18 = (bf16[8,64,128]{2,1,0:T(8,128)(2,1)}, bf16[8,64,128]{2,1,0:T(8,128)(2,1)S(1)}, u32[]{:S(2)}) copy-start(bf16[8,64,128]{2,1,0:T(8,128)(2,1)S(1)} %collective-permute-done.q01_ref) | copy-start | bytes 393220
  120.0 10.0 %collective-permute-start.2 = (bf16[8,64,128]{2,1,0:T(8,128)(2,1)S(1)}, bf16[8,64,128]{2,1,0:T(8,128)(2,1)S(1)}, u32[]{:S(2)}, u32[]{:S(2)}) collective-permute-start(bf16[8,64,128]{2,1,0:T(8,128)(2,1)S(1)} %collective-permute-done.q01_ref), channel_id=1, source_target_pairs={{0,8},{8,0},{16,24},{24,16},{32,40},{40,32},{48,56},{56,48},{64,72... | collective-permute-start | bytes 393224 | tf_op jit(solution)/shard_map/ppermute | solution.py:373
  120.1 0.8 copy-start.8
  123.2 17.3 %copy-start = (bf16[8,72,256]{2,1,0:T(8,128)(2,1)}, bf16[8,72,256]{2,1,0:T(8,128)(2,1)S(1)}, u32[]{:S(2)}) copy-start(bf16[8,72,256]{2,1,0:T(8,128)(2,1)S(1)} %all-to-all-done.6.in_ref) | copy-start | bytes 884740
  123.2 31.2 %all-to-all-start.4 = ((bf16[8,72,256]{2,1,0:T(8,128)(2,1)}), bf16[8,72,256]{2,1,0:T(8,128)(2,1)S(1)}, u32[]{:S(2)}, u32[]{:S(2)}) async-start(bf16[8,72,256]{2,1,0:T(8,128)(2,1)} %sides.4), calls=%async_computation.4 | async-start | bytes 589824 | tf_op jit(solution)/shard_map/all_to_all | solution.py:309
  130.0 0.7 copy-start.19
  130.7 0.7 copy-start.20
  140.5 1.9 %collective-permute-start.3 = (bf16[8,136,128]{2,1,0:T(8,128)(2,1)}, bf16[8,136,128]{2,1,0:T(8,128)(2,1)S(1)}, u32[]{:S(2)}, u32[]{:S(2)}) collective-permute-start(bf16[8,136,128]{2,1,0:T(8,128)(2,1)} %get-tuple-element.26), channel_id=1, source_target_pairs={{0,8},{8,0},{16,24},{24,16},{32,40},{40,32},{48,56},{56,48},{64,72... | collective-permute-start | bytes 835592 | tf_op jit(solution)/shard_map/ppermute | solution.py:375
  142.4 0.7 copy-start.10
  145.5 6.2 %collective-permute-start.4 = (bf16[8,72,128]{2,1,0:T(8,128)(2,1)}, bf16[8,72,128]{2,1,0:T(8,128)(2,1)S(1)}, u32[]{:S(2)}, u32[]{:S(2)}) collective-permute-start(bf16[8,72,128]{2,1,0:T(8,128)(2,1)} %get-tuple-element.28), channel_id=1, source_target_pairs={{0,16},{8,24},{16,0},{24,8},{32,48},{40,56},{48,32},{56,40},{64,80... | collective-permute-start | bytes 442376 | tf_op jit(solution)/shard_map/ppermute | solution.py:377
  151.7 0.7 copy-start.17
  154.4 9.1 %copy-start.1 = (bf16[8,72,256]{2,1,0:T(8,128)(2,1)}, bf16[8,72,256]{2,1,0:T(8,128)(2,1)S(1)}, u32[]{:S(2)}) copy-start(bf16[8,72,256]{2,1,0:T(8,128)(2,1)S(1)} %all-to-all-done.4.in_ref) | copy-start | bytes 884740
  154.4 16.4 %all-to-all-start.2 = ((bf16[8,72,128]{2,1,0:T(8,128)(2,1)}), bf16[8,72,128]{2,1,0:T(8,128)(2,1)S(1)}, u32[]{:S(2)}, u32[]{:S(2)}) async-start(bf16[8,72,128]{2,1,0:T(8,128)(2,1)} %sides.3), calls=%async_computation.2 | async-start | bytes 294912 | tf_op jit(solution)/shard_map/all_to_all | solution.py:309
  170.8 0.7 copy-start.4

commit v3 on v0

v3 whole, which is shorter than its diff:
```python
import functools
import math

import jax
import jax.numpy as jnp
from jax import lax
from jax.experimental import pallas as pl
from jax.experimental.pallas import tpu as pltpu
from jax.sharding import PartitionSpec as P

HDIM = 128
GROUPS = 2
NEWTOK = 256
EPSILON = 1e-06
MASKED = -1e30
STAT_ROWS = 8


def pieces(values):
    high = values.astype(jnp.bfloat16)
    rest = values - high.astype(jnp.float32)
    middle = rest.astype(jnp.bfloat16)
    low = (rest - middle.astype(jnp.float32)).astype(jnp.bfloat16)
    return high, middle, low


def to_columns(rows):
    count = rows.shape[0]
    if count < 128:
        rows = jnp.concatenate([rows, jnp.zeros((128 - count, 128), jnp.float32)], axis=0)
    return rows.T


def sums_kernel(q_ref, k_ref, out_ref):
    tokens = q_ref.shape[0]
    query = q_ref[...].astype(jnp.float32)
    key = k_ref[...].astype(jnp.float32)
    query_sum = jnp.sum(query * query, axis=1, keepdims=True)
    key_sum = jnp.sum(key * key, axis=1, keepdims=True)
    lane = lax.broadcasted_iota(jnp.int32, (tokens, 128), 1)
    both = jnp.where(lane == 0, query_sum, jnp.where(lane == 1, key_sum, 0.0))
    padded = jnp.concatenate([both, jnp.zeros((128 - tokens, 128), jnp.float32)], axis=0)
    rows = padded.T[0:8]
    for index in range(out_ref.shape[0]):
        out_ref[index] = rows


def norm_kernel(q_ref, k_ref, v_ref, qg_ref, kg_ref, sums_ref, q_out, kv_out, *, full_width, scale):
    tokens = q_ref.shape[0]
    total = sums_ref[0]
    for index in range(1, sums_ref.shape[0]):
        total = total + sums_ref[index]
    inverse = to_columns(lax.rsqrt(total / full_width + EPSILON))
    query_inverse = inverse[0:tokens, 0:1]
    key_inverse = inverse[0:tokens, 1:2]
    q_out[...] = (
        q_ref[...].astype(jnp.float32) * query_inverse * (qg_ref[...] * scale)
    ).astype(jnp.bfloat16)
    kv_out[0] = (
        k_ref[...].astype(jnp.float32) * key_inverse * kg_ref[...]
    ).astype(jnp.bfloat16)
    kv_out[1] = v_ref[...]


def bias_kernel(length_ref, place_ref, table_ref, bias_ref, *, pages, page_len):
    lane = lax.broadcasted_iota(jnp.int32, (1, page_len), 1)
    page_ids = lax.broadcasted_iota(jnp.int32, (1, table_ref.shape[1]), 1)
    for group in range(GROUPS):
        table_row = table_ref[group : group + 1, :]
        for core in range(2):
            for page in range(pages):
                slot = (place_ref[core] * GROUPS + group) * pages + page
                logical = jnp.sum(
                    jnp.where(table_row == slot, page_ids, 0), axis=1, keepdims=True
                )
                usable = logical * page_len + lane < length_ref[group]
                column = (core * pages + page) * page_len
                bias_ref[group, :, column : column + page_len] = jnp.where(usable, 0.0, MASKED)


def read_lse(ref, rows):
    found = []
    for first in range(0, ref.shape[1], HDIM):
        block = ref[rows : rows + STAT_ROWS, first : first + HDIM].astype(jnp.float32)
        found.append(block[0:1] + block[1:2] + block[2:3])
    return jnp.concatenate(found, axis=0)


def write_lse(ref, rows, lse):
    row = lax.broadcasted_iota(jnp.int32, (STAT_ROWS, 128), 0)
    for head in range(lse.shape[0]):
        high, middle, low = (
            piece.astype(jnp.float32) for piece in pieces(lse[head : head + 1])
        )
        block = jnp.where(
            row == 0, high, jnp.where(row == 1, middle, jnp.where(row == 2, low, 0.0))
        )
        ref[rows : rows + STAT_ROWS, head * HDIM : (head + 1) * HDIM] = block.astype(jnp.bfloat16)


def transposed_dot(left, right):
    return lax.dot_general(
        left, right, (((1,), (1,)), ((), ())), preferred_element_type=jnp.float32
    )


def attend_kernel(
    group_ref, length_ref, request_ref, bias_ref, *refs, count, own, pages, page_len, capacity
):
    query_refs, refs = refs[:count], refs[count:]
    cache_refs, refs = (refs[0:2], refs[2:4]), refs[4:]
    if own:
        own_refs, refs = refs[:2], refs[2:]
    out_refs, stats_ref = refs[:count], refs[count]
    head = pl.program_id(0)
    heads = out_refs[0].shape[1] // HDIM
    rows = query_refs[0].shape[0]
    cached = pages * page_len
    here = pl.ds(pl.multiple_of(head * HDIM, HDIM), HDIM)
    lane = lax.broadcasted_iota(jnp.int32, (rows, 128), 1)

    def run(index, group, masked):
        query = query_refs[index][...]
        scores = []
        for core, (key_ref, _) in enumerate(cache_refs):
            keys = key_ref[pl.ds(group * pages, pages)].reshape(cached, HDIM)
            part = transposed_dot(query, keys)
            if masked:
                part = part + bias_ref[group, :, core * cached : (core + 1) * cached]
            scores.append(part)
        values = [
            value_ref[pl.ds(group * pages, pages)].reshape(cached, HDIM)
            for _, value_ref in cache_refs
        ]
        if own:
            scores.append(
                transposed_dot(query, jnp.concatenate([ref[0] for ref in own_refs], axis=0))
            )
            values.append(jnp.concatenate([ref[1] for ref in own_refs], axis=0))
        top = functools.reduce(
            jnp.maximum, [jnp.max(part, axis=1, keepdims=True) for part in scores]
        )
        total = None
        mixed = None
        for part, value in zip(scores, values):
            weights = jnp.exp2(part - top)
            more = jnp.sum(weights, axis=1, keepdims=True)
            term = jnp.dot(weights.astype(jnp.bfloat16), value, preferred_element_type=jnp.float32)
            total = more if total is None else total + more
            mixed = term if mixed is None else mixed + term
        out_refs[index][0:rows, here] = (mixed * (1.0 / total)).astype(jnp.bfloat16)
        stats_ref[index] = jnp.where(lane == head, top + jnp.log2(total), stats_ref[index])

    for index in range(count):
        group = group_ref[request_ref[index]]
        if own:
            run(index, group, True)
        else:
            full = length_ref[group] == capacity
            pl.when(full)(functools.partial(run, index, group, False))
            pl.when(jnp.logical_not(full))(functools.partial(run, index, group, True))

    @pl.when(head == heads - 1)
    def _():
        for index in range(count):
            write_lse(out_refs[index], rows, stats_ref[index].T[0:heads])


def merge_weights(stats):
    top = functools.reduce(jnp.maximum, stats)
    weights = [jnp.exp2(stat - top) for stat in stats]
    total = functools.reduce(jnp.add, weights)
    return [weight / total for weight in weights], top + jnp.log2(total)


def weighted(refs, rows, weights, head):
    heads = refs[0].shape[1] // HDIM
    here = slice(head * HDIM, (head + 1) * HDIM)
    merged = None
    for index, ref in enumerate(refs):
        lane = index * heads + head
        term = ref[0:rows, here].astype(jnp.float32) * weights[0:rows, lane : lane + 1]
        merged = term if merged is None else merged + term
    return merged.astype(jnp.bfloat16)


def gather_kernel(*refs):
    in_refs, (keep_ref, send_ref) = refs[:-2], refs[-2:]
    rows = in_refs[0].shape[0] - STAT_ROWS
    half = rows // 2
    weights, lse = merge_weights([read_lse(ref, rows) for ref in in_refs])
    columns = to_columns(jnp.concatenate(weights, axis=0))
    for head in range(lse.shape[0]):
        here = slice(head * HDIM, (head + 1) * HDIM)
        merged = weighted(in_refs, rows, columns, head)
        keep_ref[0:half, here] = merged[0:half]
        send_ref[0:half, here] = merged[half:]
    write_lse(keep_ref, half, lse)
    write_lse(send_ref, half, jnp.concatenate([lse[:, half:], lse[:, 0:half]], axis=1))


def last_kernel(one_ref, two_ref, out_ref):
    rows = out_ref.shape[0]
    weights, lse = merge_weights([read_lse(ref, rows) for ref in (one_ref, two_ref)])
    columns = to_columns(jnp.concatenate(weights, axis=0))
    for head in range(lse.shape[0]):
        out_ref[:, head * HDIM : (head + 1) * HDIM] = weighted(
            (one_ref, two_ref), rows, columns, head
        )


def on_device(
    q_raw,
    k_raw,
    v_new,
    q_gain,
    k_gain,
    cache_keys,
    cache_values,
    page_table,
    cached_lengths,
    req_group,
):
    tok_dev, width = q_raw.shape
    tp_count = lax.axis_size("tp")
    seq_count = lax.axis_size("seq")
    heads = width // HDIM
    page_len = cache_keys.shape[1]
    pages = cache_keys.shape[0] // GROUPS
    requests = req_group.shape[0]
    plane = seq_count // requests
    seq_index = lax.axis_index("seq")
    z_index = seq_index // plane
    bf16 = jnp.bfloat16
    f32 = jnp.float32
    scale = math.log2(math.e) / math.sqrt(HDIM)
    rows = 2 * tok_dev
    chunk = rows + STAT_ROWS
    cached = 2 * pages * page_len

    def along_z(array, distance):
        pairs = [(index, (index + distance * plane) % seq_count) for index in range(seq_count)]
        return lax.ppermute(array, "seq", pairs)

    def across(array, bit):
        return lax.ppermute(array, "seq", [(index, index ^ bit) for index in range(seq_count)])

    sums = pl.pallas_call(
        sums_kernel, out_shape=jax.ShapeDtypeStruct((tp_count, 8, 128), f32), name="sums"
    )(q_raw, k_raw)
    sums = lax.all_to_all(sums, "tp", split_axis=0, concat_axis=0, tiled=True)
    other_keys = across(cache_keys, 1)
    other_values = across(cache_values, 1)
    queries, own_kv = pl.pallas_call(
        functools.partial(norm_kernel, full_width=float(width * tp_count), scale=scale),
        out_shape=(
            jax.ShapeDtypeStruct((tok_dev, width), bf16),
            jax.ShapeDtypeStruct((2, tok_dev, width), bf16),
        ),
        name="norm",
    )(q_raw, k_raw, v_new, q_gain[None, :], k_gain[None, :], sums)
    other_kv = across(own_kv, 1)
    mine = jnp.concatenate([queries, across(queries, 2)], axis=0)

    places = jnp.stack([seq_index, seq_index ^ 1]).astype(jnp.int32)
    smem = pl.BlockSpec(memory_space=pltpu.SMEM)
    bias = pl.pallas_call(
        functools.partial(bias_kernel, pages=pages, page_len=page_len),
        out_shape=jax.ShapeDtypeStruct((GROUPS, 1, cached), f32),
        in_specs=[smem, smem, pl.BlockSpec(memory_space=pltpu.VMEM)],
        name="bias",
    )(cached_lengths, places, page_table)

    def attend(arrays, offsets, own):
        count = len(arrays)
        ids = jnp.stack([(z_index + offset) % requests for offset in offsets]).astype(jnp.int32)
        whole = lambda shape: pl.BlockSpec(shape, lambda h, *_: (0,) * len(shape))
        cache_spec = pl.BlockSpec((GROUPS * pages, page_len, HDIM), lambda h, *_: (0, 0, h))
        own_spec = pl.BlockSpec((2, tok_dev, HDIM), lambda h, *_: (0, 0, h))
        return pl.pallas_call(
            functools.partial(
                attend_kernel,
                count=count,
                own=own,
                pages=pages,
                page_len=page_len,
                capacity=page_table.shape[1] * page_len,
            ),
            out_shape=(jax.ShapeDtypeStruct((chunk, width), bf16),) * count,
            grid_spec=pltpu.PrefetchScalarGridSpec(
                num_scalar_prefetch=3,
                grid=(heads,),
                in_specs=[whole((GROUPS, 1, cached))]
                + [pl.BlockSpec((rows, HDIM), lambda h, *_: (0, h))] * count
                + [cache_spec] * 4
                + ([own_spec] * 2 if own else []),
                out_specs=(whole((chunk, width)),) * count,
                scratch_shapes=[pltpu.VMEM((count, rows, 128), f32)],
            ),
            name="attend",
        )(
            req_group,
            cached_lengths,
            ids,
            bias,
            *arrays,
            cache_keys,
            cache_values,
            other_keys,
            other_values,
            *((own_kv, other_kv) if own else ()),
        )

    steps = requests // 2
    below = above = mine
    arrived = []
    for step in range(1, steps + 1):
        below = along_z(below, 1)
        if step < requests - step:
            above = along_z(above, -1)
            arrived.append(((below, above), (-step, step)))
        else:
            arrived.append(((below,), (-step,)))
    partials = list(attend((mine,), (0,), True))
    for arrays, offsets in arrived:
        for result, offset in zip(attend(arrays, offsets, False), offsets):
            partials.append(along_z(result, offset))
    small = jax.ShapeDtypeStruct((tok_dev + STAT_ROWS, width), bf16)
    keep, send = pl.pallas_call(gather_kernel, out_shape=(small, small), name="gather")(*partials)
    return pl.pallas_call(
        last_kernel, out_shape=jax.ShapeDtypeStruct((tok_dev, width), bf16), name="last"
    )(keep, across(send, 2))


def solution(mesh):
    return jax.shard_map(
        on_device,
        mesh=mesh,
        in_specs=(
            P("seq", "tp"),
            P("seq", "tp"),
            P("seq", "tp"),
            P("tp"),
            P("tp"),
            P("seq", None, "tp"),
            P("seq", None, "tp"),
            P(),
            P(),
            P(),
        ),
        out_specs=P("seq", "tp"),
        check_vma=False,
    )
```

time: 393 us -> 136 us (0.35); the launches traced: 388 us -> 135 us
  local copies, waits for them, and re-layouts: 122 us -> 7.6 us
  waiting for transfers between devices: 119 us -> 31 us
  Pallas kernels: 0 us -> 60.2 us
  other arithmetic: 49.6 us -> 2.37 us
  matrix products: 36.8 us -> 0 us
  blocking collectives: 24.3 us -> 0 us
  between operations: 13.7 us -> 0.18 us
  starting transfers between devices: 22.2 us -> 33.9 us
    all_to_all x3 -> x1, waiting for transfers between devices: 104 us -> 5.16 us  [on_device(): sums = lax.all_to_all(sums, 'tp', split_axis=0, concat_axis=0, tiled=True)]
    pallas_call x0 -> x10, Pallas kernels: none -> 60.2 us  [the longest x5 50.2 us: attend(): pl.pallas_call(functools.partial(attend_kernel, count=count, own=own, pag...]
    gather x5 -> x0, local copies, waits for them, and re-layouts: 39 us -> none  [the longest x1 12.4 us: on_device(): token_mix = jnp.take(joined_mix, placement_rows, axis=0)]
    dot_general x8 -> x0, matrix products: 36.8 us -> none  [the longest x4 23.4 us: attend(): jnp.einsum('hqk,khd->qhd', weights.astype(jnp.bfloat16), values_all, pref...]
    ppermute x0 -> x19, starting transfers between devices: none -> 26.9 us  [the longest x14 25.1 us: along_z(): return lax.ppermute(array, 'seq', pairs)]
    ppermute x0 -> x19, waiting for transfers between devices: none -> 25.8 us  [the longest x14 18.7 us: along_z(): return lax.ppermute(array, 'seq', pairs)]
    psum x1 -> x0, blocking collectives: 24.3 us -> none  [on_device(): lax.psum((jnp.sum(raw_query * raw_query, axis=1), jnp.sum(raw_key * raw_k...]
    reduce_sum x11 -> x0, other arithmetic: 17.8 us -> none  [the longest x4 10.7 us: attend(): totals = jnp.sum(weights, axis=2)]
  transfers between devices with their start and end apart: 4 -> 20, of which waited for: 3 -> 8; matrix products, arithmetic and copies ran while one was open for 22% -> 4% of each run, Pallas kernels for 0% -> 41%
where the time goes in v3:
time: 136 us; the launch traced here: 135 us
  Pallas kernels  60.2 us (44%)
  starting transfers between devices  33.9 us (25%)
  waiting for transfers between devices  31 us (23%)
  local copies, waits for them, and re-layouts  7.6 us (6%)
  other arithmetic  2.37 us (2%)
    pallas_call x5, Pallas kernels, attend(): pl.pallas_call(functools.partial(attend_kernel, count=count, own=own, pag...  50.2 us
    ppermute x14, starting transfers between devices, along_z(): return lax.ppermute(array, 'seq', pairs)  25.1 us
    ppermute x14, waiting for transfers between devices, along_z(): return lax.ppermute(array, 'seq', pairs)  18.7 us
    ppermute x5, waiting for transfers between devices, across(): lax.ppermute(array, 'seq', [(index, index ^ bit) for index in range(seq_c...  7.13 us
    all_to_all x1, starting transfers between devices, on_device(): sums = lax.all_to_all(sums, 'tp', split_axis=0, concat_axis=0, tiled=True)  6.93 us
    all_to_all x1, waiting for transfers between devices, on_device(): sums = lax.all_to_all(sums, 'tp', split_axis=0, concat_axis=0, tiled=True)  5.16 us
    unnamed x39, local copies, waits for them, and re-layouts  5.02 us
    pallas_call x1, Pallas kernels, on_device(): pl.pallas_call(gather_kernel, out_shape=(small, small), name='gather')  3.11 us
  transfers between devices with their start and end apart: 20, of which 8 were waited for; matrix products, arithmetic and copies ran while one was open for 4% of the time, Pallas kernels for 41%

profile of v3, /device:TPU:64, one launch (start us, length us, event | category | flops | bytes accessed | tf_op | source)
XLA Modules:
  0.0 135.2 jit_solution(8157307811255619393)
XLA Ops:
  0.0 0.5 collective-permute-start.2
  0.5 1.7 %sums.1 = f32[8,8,128]{2,1,0:T(8,128)} custom-call(bf16[64,640]{1,0:T(8,128)(2,1)} %q_ref.3, bf16[64,640]{1,0:T(8,128)(2,1)} %k_ref.3), custom_call_target="tpu_custom_call" | custom-call | tf_op jit(solution)/shard_map/sums/pallas_call | solution.py:248
  2.2 6.9 %all-to-all-start = ((f32[8,8,128]{2,1,0:T(8,128)}), f32[8,8,128]{2,1,0:T(8,128)S(1)}, u32[]{:S(2)}, u32[]{:S(2)}) async-start(f32[8,8,128]{2,1,0:T(8,128)} %sums.1), calls=%async_computation | async-start | bytes 65536 | tf_op jit(solution)/shard_map/all_to_all | solution.py:251
  9.1 1.3 broadcast_in_dim.6.qg_ref
  10.4 1.3 broadcast_in_dim.7.kg_ref
  11.7 5.2 %all-to-all-done.sums_ref = f32[8,8,128]{2,1,0:T(8,128)S(1)} async-done(((f32[8,8,128]{2,1,0:T(8,128)}), f32[8,8,128]{2,1,0:T(8,128)S(1)}, u32[]{:S(2)}, u32[]{:S(2)}) %all-to-all-start) | async-done | bytes 32800 | tf_op jit(solution)/shard_map/all_to_all | solution.py:251
  16.9 0.6 copy-done.14
  17.5 1.9 %norm.1 = (bf16[64,640]{1,0:T(8,128)(2,1)}, bf16[2,64,640]{2,1,0:T(8,128)(2,1)}) custom-call(bf16[64,640]{1,0:T(8,128)(2,1)} %q_ref.3, bf16[64,640]{1,0:T(8,128)(2,1)} %k_ref.3, bf16[64,640]{1,0:T(8,128)(2,1)} %v_ref.1, f32[1,640]{1,0:T(1,128)} %broadcast_in_dim.6.qg_ref, f32[1,640]{1,0:T(1,128)} %broadcast_in_dim.7.kg_ref, f32[8,8,128]{2,1,0:T(8,128)} %copy-done.14), custom_call_target="tpu_custom_call" | custom-call | tf_op jit(solution)/shard_map/norm/pallas_call | solution.py:254
  19.3 0.7 collective-permute-start
  20.0 0.9 constant_dynamic-update-slice_fusion.1
  20.9 3.0 %collective-permute-done = bf16[64,640]{1,0:T(8,128)(2,1)S(1)} collective-permute-done((bf16[64,640]{1,0:T(8,128)(2,1)}, bf16[64,640]{1,0:T(8,128)(2,1)S(1)}, u32[]{:S(2)}, u32[]{:S(2)}) %collective-permute-start) | collective-permute-done | bytes 81952 | tf_op jit(solution)/shard_map/ppermute | solution.py:246
  24.0 2.0 %collective-permute-start.4 = (bf16[128,640]{1,0:T(8,128)(2,1)S(1)}, bf16[128,640]{1,0:T(8,128)(2,1)S(1)}, u32[]{:S(2)}, u32[]{:S(2)}) collective-permute-start(bf16[128,640]{1,0:T(8,128)(2,1)S(1)} %constant_dynamic-update-slice_fusion.refs_0_), channel_id=1, source_target_pairs={{0,32},{8,40},{16,48},{24,56},{32,64},{40,72},{48,80},{56,88},{64,... | collective-permute-start | bytes 491528 | tf_op jit(solution)/shard_map/ppermute | solution.py:243
  26.0 0.1 collective-permute-start.5
  26.1 4.4 %collective-permute-done.4.refs_0_ = bf16[128,640]{1,0:T(8,128)(2,1)S(1)} collective-permute-done((bf16[128,640]{1,0:T(8,128)(2,1)S(1)}, bf16[128,640]{1,0:T(8,128)(2,1)S(1)}, u32[]{:S(2)}, u32[]{:S(2)}) %collective-permute-start.4) | collective-permute-done | bytes 163872 | tf_op jit(solution)/shard_map/ppermute | solution.py:243
  30.5 1.4 %collective-permute-start.8 = (bf16[128,640]{1,0:T(8,128)(2,1)S(1)}, bf16[128,640]{1,0:T(8,128)(2,1)S(1)}, u32[]{:S(2)}, u32[]{:S(2)}) collective-permute-start(bf16[128,640]{1,0:T(8,128)(2,1)S(1)} %collective-permute-done.4.refs_0_), channel_id=1, source_target_pairs={{0,32},{8,40},{16,48},{24,56},{32,64},{40,72},{48,80},{56,88},{64,... | collective-permute-start | bytes 491528 | tf_op jit(solution)/shard_map/ppermute | solution.py:243
  32.0 0.6 collective-permute-done.5.refs_1_
  32.5 0.0 collective-permute-start.9
  32.6 4.9 %collective-permute-done.8.refs_0_ = bf16[128,640]{1,0:T(8,128)(2,1)S(1)} collective-permute-done((bf16[128,640]{1,0:T(8,128)(2,1)S(1)}, bf16[128,640]{1,0:T(8,128)(2,1)S(1)}, u32[]{:S(2)}, u32[]{:S(2)}) %collective-permute-start.8) | collective-permute-done | bytes 163872 | tf_op jit(solution)/shard_map/ppermute | solution.py:243
  37.5 2.1 %collective-permute-start.12 = (bf16[128,640]{1,0:T(8,128)(2,1)S(1)}, bf16[128,640]{1,0:T(8,128)(2,1)S(1)}, u32[]{:S(2)}, u32[]{:S(2)}) collective-permute-start(bf16[128,640]{1,0:T(8,128)(2,1)S(1)} %collective-permute-done.8.refs_0_), channel_id=1, source_target_pairs={{0,32},{8,40},{16,48},{24,56},{32,64},{40,72},{48,80},{56,88},{64,... | collective-permute-start | bytes 491528 | tf_op jit(solution)/shard_map/ppermute | solution.py:243
  39.6 0.6 pad_add_fusion.place_ref
  40.2 1.5 %bias.1.bias_ref = f32[2,1,2048]{2,1,0:T(1,128)} custom-call(s32[2]{0:T(128)} %length_ref.11, s32[2]{0:T(128)} %pad_add_fusion.place_ref, s32[2,256]{1,0:T(2,128)} %table_ref.1), custom_call_target="tpu_custom_call" | custom-call | tf_op jit(solution)/shard_map/bias/pallas_call | solution.py:267
  41.6 0.6 pad_add_fusion.1.request_ref
  42.2 0.1 collective-permute-start.13
  42.3 0.5 collective-permute-done.12.refs_0_
  42.8 3.3 %collective-permute-start.16 = (bf16[128,640]{1,0:T(8,128)(2,1)S(1)}, bf16[128,640]{1,0:T(8,128)(2,1)}, u32[]{:S(2)}, u32[]{:S(2)}) collective-permute-start(bf16[128,640]{1,0:T(8,128)(2,1)S(1)} %collective-permute-done.12.refs_0_), channel_id=1, source_target_pairs={{0,32},{8,40},{16,48},{24,56},{32,64},{40,72},{48,80},{56,88},{64,... | collective-permute-start | bytes 491528 | tf_op jit(solution)/shard_map/ppermute | solution.py:243
  46.1 1.5 %copy-done = bf16[16,128,640]{2,1,0:T(8,128)(2,1)} copy-done((bf16[16,128,640]{2,1,0:T(8,128)(2,1)}, bf16[16,128,640]{2,1,0:T(8,128)(2,1)S(1)}, u32[]{:S(2)}) %copy-start) | copy-done | bytes 2621464
  47.6 10.8 %attend.6 = (bf16[136,640]{1,0:T(8,128)(2,1)}, bf16[136,640]{1,0:T(8,128)(2,1)}) custom-call(s32[8]{0:T(128)} %group_ref.9, s32[2]{0:T(128)} %length_ref.11, s32[2]{0:T(128)} %pad_add_fusion.1.request_ref, f32[2,1,2048]{2,1,0:T(1,128)} %bias.1.bias_ref, bf16[128,640]{1,0:T(8,128)(2,1)} %copy-done.13, bf16[128,640]{1,0:T(8,128)(2,1)} %collective-permute-done.5.refs_1_, ...), custom_call_target="tpu_custom_call" | custom-call | tf_op jit(solution)/shard_map/attend/pallas_call | solution.py:280
  58.4 0.1 collective-permute-start.6
  58.5 3.9 %collective-permute-start.7 = (bf16[136,640]{1,0:T(8,128)(2,1)}, bf16[136,640]{1,0:T(8,128)(2,1)S(1)}, u32[]{:S(2)}, u32[]{:S(2)}) collective-permute-start(bf16[136,640]{1,0:T(8,128)(2,1)} %get-tuple-element.18), channel_id=1, source_target_pairs={{0,32},{8,40},{16,48},{24,56},{32,64},{40,72},{48,80},{56,88},{64,... | collective-permute-start | bytes 522248 | tf_op jit(solution)/shard_map/ppermute | solution.py:243
  62.4 0.6 pad_add_fusion.2.request_ref
  63.1 0.6 pad_add_fusion.3.request_ref
  63.6 10.8 %attend.7 = (bf16[136,640]{1,0:T(8,128)(2,1)}, bf16[136,640]{1,0:T(8,128)(2,1)}) custom-call(s32[8]{0:T(128)} %group_ref.9, s32[2]{0:T(128)} %length_ref.11, s32[2]{0:T(128)} %pad_add_fusion.2.request_ref, f32[2,1,2048]{2,1,0:T(1,128)} %bias.1.bias_ref, bf16[128,640]{1,0:T(8,128)(2,1)} %copy-done.9, bf16[128,640]{1,0:T(8,128)(2,1)} %copy-done.11, ...), custom_call_target="tpu_custom_call" | custom-call | tf_op jit(solution)/shard_map/attend/pallas_call | solution.py:280
  74.4 0.1 collective-permute-start.10
  74.5 10.8 %attend.8 = (bf16[136,640]{1,0:T(8,128)(2,1)}, bf16[136,640]{1,0:T(8,128)(2,1)}) custom-call(s32[8]{0:T(128)} %group_ref.9, s32[2]{0:T(128)} %length_ref.11, s32[2]{0:T(128)} %pad_add_fusion.3.request_ref, f32[2,1,2048]{2,1,0:T(1,128)} %bias.1.bias_ref, bf16[128,640]{1,0:T(8,128)(2,1)} %copy-done.10, bf16[128,640]{1,0:T(8,128)(2,1)} %collective-permute-done.13.refs_1_, ...), custom_call_target="tpu_custom_call" | custom-call | tf_op jit(solution)/shard_map/attend/pallas_call | solution.py:280
  85.4 4.2 %collective-permute-start.11 = (bf16[136,640]{1,0:T(8,128)(2,1)S(1)}, bf16[136,640]{1,0:T(8,128)(2,1)S(1)}, u32[]{:S(2)}, u32[]{:S(2)}) collective-permute-start(bf16[136,640]{1,0:T(8,128)(2,1)S(1)} %copy-done.16), channel_id=1, source_target_pairs={{0,64},{8,72},{16,80},{24,88},{32,96},{40,104},{48,112},{56,120},{... | collective-permute-start | bytes 522248 | tf_op jit(solution)/shard_map/ppermute | solution.py:243
  89.6 8.8 %attend.9 = bf16[136,640]{1,0:T(8,128)(2,1)} custom-call(s32[8]{0:T(128)} %group_ref.9, s32[2]{0:T(128)} %length_ref.11, s32[1]{0:T(128)} %bitcast.9.request_ref, f32[2,1,2048]{2,1,0:T(1,128)} %bias.1.bias_ref, bf16[128,640]{1,0:T(8,128)(2,1)} %collective-permute-done.16.refs_0_, bf16[16,128,640]{2,1,0:T(8,128)(2,1)} %refs_1_.3, ...), custom_call_target="tpu_custom_call" | custom-call | tf_op jit(solution)/shard_map/attend/pallas_call | solution.py:280
  98.4 2.6 %collective-permute-start.14 = (bf16[136,640]{1,0:T(8,128)(2,1)S(1)}, bf16[136,640]{1,0:T(8,128)(2,1)S(1)}, u32[]{:S(2)}, u32[]{:S(2)}) collective-permute-start(bf16[136,640]{1,0:T(8,128)(2,1)S(1)} %copy-done.18), channel_id=1, source_target_pairs={{0,160},{8,168},{16,176},{24,184},{32,192},{40,200},{48,208},{56,2... | collective-permute-start | bytes 522248 | tf_op jit(solution)/shard_map/ppermute | solution.py:243
  101.1 2.6 %collective-permute-start.15 = (bf16[136,640]{1,0:T(8,128)(2,1)S(1)}, bf16[136,640]{1,0:T(8,128)(2,1)S(1)}, u32[]{:S(2)}, u32[]{:S(2)}) collective-permute-start(bf16[136,640]{1,0:T(8,128)(2,1)S(1)} %copy-done.17), channel_id=1, source_target_pairs={{0,96},{8,104},{16,112},{24,120},{32,128},{40,136},{48,144},{56,15... | collective-permute-start | bytes 522248 | tf_op jit(solution)/shard_map/ppermute | solution.py:243
  103.6 2.5 %collective-permute-start.17 = (bf16[136,640]{1,0:T(8,128)(2,1)}, bf16[136,640]{1,0:T(8,128)(2,1)S(1)}, u32[]{:S(2)}, u32[]{:S(2)}) collective-permute-start(bf16[136,640]{1,0:T(8,128)(2,1)} %attend.9), channel_id=1, source_target_pairs={{0,128},{8,136},{16,144},{24,152},{32,160},{40,168},{48,176},{56,1... | collective-permute-start | bytes 522248 | tf_op jit(solution)/shard_map/ppermute | solution.py:243
  106.2 8.9 %attend.5.refs_0_ = bf16[136,640]{1,0:T(8,128)(2,1)} custom-call(s32[8]{0:T(128)} %group_ref.9, s32[2]{0:T(128)} %length_ref.11, s32[1]{0:T(128)} %bitcast.request_ref, f32[2,1,2048]{2,1,0:T(1,128)} %bias.1.bias_ref, bf16[128,640]{1,0:T(8,128)(2,1)} %copy-done.1, bf16[16,128,640]{2,1,0:T(8,128)(2,1)} %refs_1_.3, bf16[16,128,640]{2,1,0:T(8,128)(2,1)} %refs_2_.9, ...), custom_call_target="tpu_custom_call" | custom-call | tf_op jit(solution)/shard_map/attend/pallas_call | solution.py:280
  115.2 8.3 %collective-permute-done.15.refs_6_ = bf16[136,640]{1,0:T(8,128)(2,1)S(1)} collective-permute-done((bf16[136,640]{1,0:T(8,128)(2,1)S(1)}, bf16[136,640]{1,0:T(8,128)(2,1)S(1)}, u32[]{:S(2)}, u32[]{:S(2)}) %collective-permute-start.15) | collective-permute-done | bytes 174112 | tf_op jit(solution)/shard_map/ppermute | solution.py:243
  123.5 0.6 copy-done.7
  124.1 0.7 copy-done.8
  124.8 3.1 %gather.1 = (bf16[72,640]{1,0:T(8,128)(2,1)}, bf16[72,640]{1,0:T(8,128)(2,1)}) custom-call(bf16[136,640]{1,0:T(8,128)(2,1)} %attend.5.refs_0_, bf16[136,640]{1,0:T(8,128)(2,1)} %copy-done.2, bf16[136,640]{1,0:T(8,128)(2,1)} %copy-done.3, bf16[136,640]{1,0:T(8,128)(2,1)} %copy-done.4, bf16[136,640]{1,0:T(8,128)(2,1)} %copy-done.5, ...), custom_call_target="tpu_custom_call" | custom-call | tf_op jit(solution)/shard_map/gather/pallas_call | solution.py:329
  127.9 0.7 collective-permute-start.18
  128.6 4.1 %collective-permute-done.18.two_ref = bf16[72,640]{1,0:T(8,128)(2,1)S(1)} collective-permute-done((bf16[72,640]{1,0:T(8,128)(2,1)}, bf16[72,640]{1,0:T(8,128)(2,1)S(1)}, u32[]{:S(2)}, u32[]{:S(2)}) %collective-permute-start.18) | collective-permute-done | bytes 92192 | tf_op jit(solution)/shard_map/ppermute | solution.py:246
  132.7 0.6 copy-done.15
  133.3 1.9 %last.1 = bf16[64,640]{1,0:T(8,128)(2,1)} custom-call(bf16[72,640]{1,0:T(8,128)(2,1)} %get-tuple-element.23.one_ref, bf16[72,640]{1,0:T(8,128)(2,1)} %copy-done.15), custom_call_target="tpu_custom_call" | custom-call | tf_op jit(solution)/shard_map/last/pallas_call | solution.py:330
  (48 shorter events, 0.1 us)
Async XLA Ops:
  0.0 46.1 %collective-permute-start.1 = (bf16[16,128,640]{2,1,0:T(8,128)(2,1)}, bf16[16,128,640]{2,1,0:T(8,128)(2,1)S(1)}, u32[]{:S(2)}, u32[]{:S(2)}) collective-permute-start(bf16[16,128,640]{2,1,0:T(8,128)(2,1)} %refs_1_.3), channel_id=1, source_target_pairs={{0,8},{8,0},{16,24},{24,16},{32,40},{40,32},{48,56},{56,48},{64,72... | collective-permute-start | bytes 7864328 | tf_op jit(solution)/shard_map/ppermute | solution.py:246
  0.0 46.1 %collective-permute-start.2 = (bf16[16,128,640]{2,1,0:T(8,128)(2,1)}, bf16[16,128,640]{2,1,0:T(8,128)(2,1)}, u32[]{:S(2)}, u32[]{:S(2)}) collective-permute-start(bf16[16,128,640]{2,1,0:T(8,128)(2,1)} %refs_2_.9), channel_id=1, source_target_pairs={{0,8},{8,0},{16,24},{24,16},{32,40},{40,32},{48,56},{56,48},{64,72... | collective-permute-start | bytes 7864328 | tf_op jit(solution)/shard_map/ppermute | solution.py:246
  2.2 14.7 %all-to-all-start = ((f32[8,8,128]{2,1,0:T(8,128)}), f32[8,8,128]{2,1,0:T(8,128)S(1)}, u32[]{:S(2)}, u32[]{:S(2)}) async-start(f32[8,8,128]{2,1,0:T(8,128)} %sums.1), calls=%async_computation | async-start | bytes 65536 | tf_op jit(solution)/shard_map/all_to_all | solution.py:251
  16.9 0.6 copy-start.14
  19.3 4.7 %collective-permute-start = (bf16[64,640]{1,0:T(8,128)(2,1)}, bf16[64,640]{1,0:T(8,128)(2,1)S(1)}, u32[]{:S(2)}, u32[]{:S(2)}) collective-permute-start(bf16[64,640]{1,0:T(8,128)(2,1)} %get-tuple-element.15), channel_id=1, source_target_pairs={{0,16},{8,24},{16,0},{24,8},{32,48},{40,56},{48,32},{56,40},{64,80... | collective-permute-start | bytes 245768 | tf_op jit(solution)/shard_map/ppermute | solution.py:246
  24.0 34.4 %copy-start.1 = (bf16[128,640]{1,0:T(8,128)(2,1)}, bf16[128,640]{1,0:T(8,128)(2,1)S(1)}, u32[]{:S(2)}) copy-start(bf16[128,640]{1,0:T(8,128)(2,1)S(1)} %constant_dynamic-update-slice_fusion.refs_0_) | copy-start | bytes 491524
  24.0 6.5 %collective-permute-start.4 = (bf16[128,640]{1,0:T(8,128)(2,1)S(1)}, bf16[128,640]{1,0:T(8,128)(2,1)S(1)}, u32[]{:S(2)}, u32[]{:S(2)}) collective-permute-start(bf16[128,640]{1,0:T(8,128)(2,1)S(1)} %constant_dynamic-update-slice_fusion.refs_0_), channel_id=1, source_target_pairs={{0,32},{8,40},{16,48},{24,56},{32,64},{40,72},{48,80},{56,88},{64,... | collective-permute-start | bytes 491528 | tf_op jit(solution)/shard_map/ppermute | solution.py:243
  26.0 6.5 %collective-permute-start.5 = (bf16[128,640]{1,0:T(8,128)(2,1)S(1)}, bf16[128,640]{1,0:T(8,128)(2,1)}, u32[]{:S(2)}, u32[]{:S(2)}) collective-permute-start(bf16[128,640]{1,0:T(8,128)(2,1)S(1)} %constant_dynamic-update-slice_fusion.refs_0_), channel_id=1, source_target_pairs={{0,224},{8,232},{16,240},{24,248},{32,0},{40,8},{48,16},{56,24},{6... | collective-permute-start | bytes 491528 | tf_op jit(solution)/shard_map/ppermute | solution.py:243
  30.5 2.0 %copy-start.13 = (bf16[128,640]{1,0:T(8,128)(2,1)}, bf16[128,640]{1,0:T(8,128)(2,1)S(1)}, u32[]{:S(2)}) copy-start(bf16[128,640]{1,0:T(8,128)(2,1)S(1)} %collective-permute-done.4.refs_0_) | copy-start | bytes 491524
  30.5 7.0 %collective-permute-start.8 = (bf16[128,640]{1,0:T(8,128)(2,1)S(1)}, bf16[128,640]{1,0:T(8,128)(2,1)S(1)}, u32[]{:S(2)}, u32[]{:S(2)}) collective-permute-start(bf16[128,640]{1,0:T(8,128)(2,1)S(1)} %collective-permute-done.4.refs_0_), channel_id=1, source_target_pairs={{0,32},{8,40},{16,48},{24,56},{32,64},{40,72},{48,80},{56,88},{64,... | collective-permute-start | bytes 491528 | tf_op jit(solution)/shard_map/ppermute | solution.py:243
  32.5 9.7 %collective-permute-start.9 = (bf16[128,640]{1,0:T(8,128)(2,1)}, bf16[128,640]{1,0:T(8,128)(2,1)S(1)}, u32[]{:S(2)}, u32[]{:S(2)}) collective-permute-start(bf16[128,640]{1,0:T(8,128)(2,1)} %collective-permute-done.5.refs_1_), channel_id=1, source_target_pairs={{0,224},{8,232},{16,240},{24,248},{32,0},{40,8},{48,16},{56,24},{6... | collective-permute-start | bytes 491528 | tf_op jit(solution)/shard_map/ppermute | solution.py:243
  37.5 26.1 %copy-start.9 = (bf16[128,640]{1,0:T(8,128)(2,1)}, bf16[128,640]{1,0:T(8,128)(2,1)S(1)}, u32[]{:S(2)}) copy-start(bf16[128,640]{1,0:T(8,128)(2,1)S(1)} %collective-permute-done.8.refs_0_) | copy-start | bytes 491524
  37.5 5.3 %collective-permute-start.12 = (bf16[128,640]{1,0:T(8,128)(2,1)S(1)}, bf16[128,640]{1,0:T(8,128)(2,1)S(1)}, u32[]{:S(2)}, u32[]{:S(2)}) collective-permute-start(bf16[128,640]{1,0:T(8,128)(2,1)S(1)} %collective-permute-done.8.refs_0_), channel_id=1, source_target_pairs={{0,32},{8,40},{16,48},{24,56},{32,64},{40,72},{48,80},{56,88},{64,... | collective-permute-start | bytes 491528 | tf_op jit(solution)/shard_map/ppermute | solution.py:243
  42.2 56.2 %collective-permute-start.3 = (bf16[2,64,640]{2,1,0:T(8,128)(2,1)}, bf16[2,64,640]{2,1,0:T(8,128)(2,1)S(1)}, u32[]{:S(2)}, u32[]{:S(2)}) collective-permute-start(bf16[2,64,640]{2,1,0:T(8,128)(2,1)} %get-tuple-element.16.refs_5_), channel_id=1, source_target_pairs={{0,8},{8,0},{16,24},{24,16},{32,40},{40,32},{48,56},{56,48},{64,72... | collective-permute-start | bytes 491528 | tf_op jit(solution)/shard_map/ppermute | solution.py:246
  42.2 21.4 %copy-start.11 = (bf16[128,640]{1,0:T(8,128)(2,1)}, bf16[128,640]{1,0:T(8,128)(2,1)S(1)}, u32[]{:S(2)}) copy-start(bf16[128,640]{1,0:T(8,128)(2,1)S(1)} %collective-permute-done.9.refs_1_) | copy-start | bytes 491524
  42.2 32.2 %collective-permute-start.13 = (bf16[128,640]{1,0:T(8,128)(2,1)S(1)}, bf16[128,640]{1,0:T(8,128)(2,1)}, u32[]{:S(2)}, u32[]{:S(2)}) collective-permute-start(bf16[128,640]{1,0:T(8,128)(2,1)S(1)} %collective-permute-done.9.refs_1_), channel_id=1, source_target_pairs={{0,224},{8,232},{16,240},{24,248},{32,0},{40,8},{48,16},{56,24},{6... | collective-permute-start | bytes 491528 | tf_op jit(solution)/shard_map/ppermute | solution.py:243
  42.8 31.6 %copy-start.10 = (bf16[128,640]{1,0:T(8,128)(2,1)}, bf16[128,640]{1,0:T(8,128)(2,1)S(1)}, u32[]{:S(2)}) copy-start(bf16[128,640]{1,0:T(8,128)(2,1)S(1)} %collective-permute-done.12.refs_0_) | copy-start | bytes 491524
  42.8 42.6 %collective-permute-start.16 = (bf16[128,640]{1,0:T(8,128)(2,1)S(1)}, bf16[128,640]{1,0:T(8,128)(2,1)}, u32[]{:S(2)}, u32[]{:S(2)}) collective-permute-start(bf16[128,640]{1,0:T(8,128)(2,1)S(1)} %collective-permute-done.12.refs_0_), channel_id=1, source_target_pairs={{0,32},{8,40},{16,48},{24,56},{32,64},{40,72},{48,80},{56,88},{64,... | collective-permute-start | bytes 491528 | tf_op jit(solution)/shard_map/ppermute | solution.py:243
  46.1 1.5 %copy-start = (bf16[16,128,640]{2,1,0:T(8,128)(2,1)}, bf16[16,128,640]{2,1,0:T(8,128)(2,1)S(1)}, u32[]{:S(2)}) copy-start(bf16[16,128,640]{2,1,0:T(8,128)(2,1)S(1)} %collective-permute-done.1.refs_3_.refs_4_) | copy-start | bytes 7864324
  58.4 42.6 %collective-permute-start.6 = (bf16[136,640]{1,0:T(8,128)(2,1)}, bf16[136,640]{1,0:T(8,128)(2,1)S(1)}, u32[]{:S(2)}, u32[]{:S(2)}) collective-permute-start(bf16[136,640]{1,0:T(8,128)(2,1)} %get-tuple-element.17), channel_id=1, source_target_pairs={{0,224},{8,232},{16,240},{24,248},{32,0},{40,8},{48,16},{56,24},{6... | collective-permute-start | bytes 522248 | tf_op jit(solution)/shard_map/ppermute | solution.py:243
  58.5 45.1 %collective-permute-start.7 = (bf16[136,640]{1,0:T(8,128)(2,1)}, bf16[136,640]{1,0:T(8,128)(2,1)S(1)}, u32[]{:S(2)}, u32[]{:S(2)}) collective-permute-start(bf16[136,640]{1,0:T(8,128)(2,1)} %get-tuple-element.18), channel_id=1, source_target_pairs={{0,32},{8,40},{16,48},{24,56},{32,64},{40,72},{48,80},{56,88},{64,... | collective-permute-start | bytes 522248 | tf_op jit(solution)/shard_map/ppermute | solution.py:243
  74.4 11.0 %copy-start.16 = (bf16[136,640]{1,0:T(8,128)(2,1)S(1)}, bf16[136,640]{1,0:T(8,128)(2,1)}, u32[]{:S(2)}) copy-start(bf16[136,640]{1,0:T(8,128)(2,1)} %get-tuple-element.20) | copy-start | bytes 522244
  74.4 40.7 %collective-permute-start.10 = (bf16[136,640]{1,0:T(8,128)(2,1)}, bf16[136,640]{1,0:T(8,128)(2,1)S(1)}, u32[]{:S(2)}, u32[]{:S(2)}) collective-permute-start(bf16[136,640]{1,0:T(8,128)(2,1)} %get-tuple-element.19), channel_id=1, source_target_pairs={{0,192},{8,200},{16,208},{24,216},{32,224},{40,232},{48,240},{56,2... | collective-permute-start | bytes 522248 | tf_op jit(solution)/shard_map/ppermute | solution.py:243
  85.4 29.8 %collective-permute-start.11 = (bf16[136,640]{1,0:T(8,128)(2,1)S(1)}, bf16[136,640]{1,0:T(8,128)(2,1)S(1)}, u32[]{:S(2)}, u32[]{:S(2)}) collective-permute-start(bf16[136,640]{1,0:T(8,128)(2,1)S(1)} %copy-done.16), channel_id=1, source_target_pairs={{0,64},{8,72},{16,80},{24,88},{32,96},{40,104},{48,112},{56,120},{... | collective-permute-start | bytes 522248 | tf_op jit(solution)/shard_map/ppermute | solution.py:243
  89.6 8.8 %copy-start.18 = (bf16[136,640]{1,0:T(8,128)(2,1)S(1)}, bf16[136,640]{1,0:T(8,128)(2,1)}, u32[]{:S(2)}) copy-start(bf16[136,640]{1,0:T(8,128)(2,1)} %get-tuple-element.21) | copy-start | bytes 522244
  89.6 11.5 %copy-start.17 = (bf16[136,640]{1,0:T(8,128)(2,1)S(1)}, bf16[136,640]{1,0:T(8,128)(2,1)}, u32[]{:S(2)}) copy-start(bf16[136,640]{1,0:T(8,128)(2,1)} %get-tuple-element.22) | copy-start | bytes 522244
  98.4 7.8 %copy-start.12 = (bf16[2,64,640]{2,1,0:T(8,128)(2,1)}, bf16[2,64,640]{2,1,0:T(8,128)(2,1)S(1)}, u32[]{:S(2)}) copy-start(bf16[2,64,640]{2,1,0:T(8,128)(2,1)S(1)} %collective-permute-done.3.refs_6_) | copy-start | bytes 491524
  98.4 16.7 %collective-permute-start.14 = (bf16[136,640]{1,0:T(8,128)(2,1)S(1)}, bf16[136,640]{1,0:T(8,128)(2,1)S(1)}, u32[]{:S(2)}, u32[]{:S(2)}) collective-permute-start(bf16[136,640]{1,0:T(8,128)(2,1)S(1)} %copy-done.18), channel_id=1, source_target_pairs={{0,160},{8,168},{16,176},{24,184},{32,192},{40,200},{48,208},{56,2... | collective-permute-start | bytes 522248 | tf_op jit(solution)/shard_map/ppermute | solution.py:243
  101.1 14.0 %copy-start.2 = (bf16[136,640]{1,0:T(8,128)(2,1)}, bf16[136,640]{1,0:T(8,128)(2,1)S(1)}, u32[]{:S(2)}) copy-start(bf16[136,640]{1,0:T(8,128)(2,1)S(1)} %collective-permute-done.6.refs_1_) | copy-start | bytes 522244
  101.1 22.4 %collective-permute-start.15 = (bf16[136,640]{1,0:T(8,128)(2,1)S(1)}, bf16[136,640]{1,0:T(8,128)(2,1)S(1)}, u32[]{:S(2)}, u32[]{:S(2)}) collective-permute-start(bf16[136,640]{1,0:T(8,128)(2,1)S(1)} %copy-done.17), channel_id=1, source_target_pairs={{0,96},{8,104},{16,112},{24,120},{32,128},{40,136},{48,144},{56,15... | collective-permute-start | bytes 522248 | tf_op jit(solution)/shard_map/ppermute | solution.py:243
  103.6 11.5 %copy-start.3 = (bf16[136,640]{1,0:T(8,128)(2,1)}, bf16[136,640]{1,0:T(8,128)(2,1)S(1)}, u32[]{:S(2)}) copy-start(bf16[136,640]{1,0:T(8,128)(2,1)S(1)} %collective-permute-done.7.refs_2_) | copy-start | bytes 522244
  103.6 19.8 %collective-permute-start.17 = (bf16[136,640]{1,0:T(8,128)(2,1)}, bf16[136,640]{1,0:T(8,128)(2,1)S(1)}, u32[]{:S(2)}, u32[]{:S(2)}) collective-permute-start(bf16[136,640]{1,0:T(8,128)(2,1)} %attend.9), channel_id=1, source_target_pairs={{0,128},{8,136},{16,144},{24,152},{32,160},{40,168},{48,176},{56,1... | collective-permute-start | bytes 522248 | tf_op jit(solution)/shard_map/ppermute | solution.py:243
  115.1 8.3 %copy-start.4 = (bf16[136,640]{1,0:T(8,128)(2,1)}, bf16[136,640]{1,0:T(8,128)(2,1)S(1)}, u32[]{:S(2)}) copy-start(bf16[136,640]{1,0:T(8,128)(2,1)S(1)} %collective-permute-done.10.refs_3_) | copy-start | bytes 522244
  115.1 8.3 %copy-start.5 = (bf16[136,640]{1,0:T(8,128)(2,1)}, bf16[136,640]{1,0:T(8,128)(2,1)S(1)}, u32[]{:S(2)}) copy-start(bf16[136,640]{1,0:T(8,128)(2,1)S(1)} %collective-permute-done.11.refs_4_) | copy-start | bytes 522244
  115.2 8.3 %copy-start.6 = (bf16[136,640]{1,0:T(8,128)(2,1)}, bf16[136,640]{1,0:T(8,128)(2,1)S(1)}, u32[]{:S(2)}) copy-start(bf16[136,640]{1,0:T(8,128)(2,1)S(1)} %collective-permute-done.14.refs_5_) | copy-start | bytes 522244
  123.5 0.7 copy-start.7
  124.1 0.7 copy-start.8
  127.9 4.8 %collective-permute-start.18 = (bf16[72,640]{1,0:T(8,128)(2,1)}, bf16[72,640]{1,0:T(8,128)(2,1)S(1)}, u32[]{:S(2)}, u32[]{:S(2)}) collective-permute-start(bf16[72,640]{1,0:T(8,128)(2,1)} %get-tuple-element.24), channel_id=1, source_target_pairs={{0,16},{8,24},{16,0},{24,8},{32,48},{40,56},{48,32},{56,40},{64,80... | collective-permute-start | bytes 276488 | tf_op jit(solution)/shard_map/ppermute | solution.py:246
  132.7 0.6 copy-start.15

commit v4 on v3

--- a/solution.py
+++ b/solution.py
@@ -14,6 +14,7 @@
 EPSILON = 1e-06
 MASKED = -1e30
 STAT_ROWS = 8
+SMALL = pltpu.CompilerParams(vmem_limit_bytes=8 * 1024 * 1024)
 
 
 def pieces(values):
@@ -105,8 +106,9 @@
 
 
 def attend_kernel(
-    group_ref, length_ref, request_ref, bias_ref, *refs, count, own, pages, page_len, capacity
+    group_ref, length_ref, place_ref, bias_ref, *refs, offsets, own, pages, page_len, capacity
 ):
+    count = len(offsets)
     query_refs, refs = refs[:count], refs[count:]
     cache_refs, refs = (refs[0:2], refs[2:4]), refs[4:]
     if own:
@@ -123,13 +125,13 @@
         query = query_refs[index][...]
         scores = []
         for core, (key_ref, _) in enumerate(cache_refs):
-            keys = key_ref[pl.ds(group * pages, pages)].reshape(cached, HDIM)
+            keys = key_ref[pl.ds(group * pages, pages), :, here].reshape(cached, HDIM)
             part = transposed_dot(query, keys)
             if masked:
                 part = part + bias_ref[group, :, core * cached : (core + 1) * cached]
             scores.append(part)
         values = [
-            value_ref[pl.ds(group * pages, pages)].reshape(cached, HDIM)
+            value_ref[pl.ds(group * pages, pages), :, here].reshape(cached, HDIM)
             for _, value_ref in cache_refs
         ]
         if own:
@@ -152,7 +154,7 @@
         stats_ref[index] = jnp.where(lane == head, top + jnp.log2(total), stats_ref[index])
 
     for index in range(count):
-        group = group_ref[request_ref[index]]
+        group = group_ref[lax.rem(place_ref[2] + offsets[index], group_ref.shape[0])]
         if own:
             run(index, group, True)
         else:
@@ -246,7 +248,7 @@
         return lax.ppermute(array, "seq", [(index, index ^ bit) for index in range(seq_count)])
 
     sums = pl.pallas_call(
-        sums_kernel, out_shape=jax.ShapeDtypeStruct((tp_count, 8, 128), f32), name="sums"
+        sums_kernel, out_shape=jax.ShapeDtypeStruct((tp_count, 8, 128), f32), compiler_params=SMALL, name="sums"
     )(q_raw, k_raw)
     sums = lax.all_to_all(sums, "tp", split_axis=0, concat_axis=0, tiled=True)
     other_keys = across(cache_keys, 1)
@@ -257,30 +259,34 @@
             jax.ShapeDtypeStruct((tok_dev, width), bf16),
             jax.ShapeDtypeStruct((2, tok_dev, width), bf16),
         ),
-        name="norm",
+        compiler_params=SMALL, name="norm",
     )(q_raw, k_raw, v_new, q_gain[None, :], k_gain[None, :], sums)
     other_kv = across(own_kv, 1)
     mine = jnp.concatenate([queries, across(queries, 2)], axis=0)
 
-    places = jnp.stack([seq_index, seq_index ^ 1]).astype(jnp.int32)
+    places = jnp.stack([seq_index, seq_index ^ 1, z_index]).astype(jnp.int32)
     smem = pl.BlockSpec(memory_space=pltpu.SMEM)
     bias = pl.pallas_call(
         functools.partial(bias_kernel, pages=pages, page_len=page_len),
         out_shape=jax.ShapeDtypeStruct((GROUPS, 1, cached), f32),
         in_specs=[smem, smem, pl.BlockSpec(memory_space=pltpu.VMEM)],
-        name="bias",
+        compiler_params=SMALL, name="bias",
     )(cached_lengths, places, page_table)
+
+    caches = [
+        pltpu.with_memory_space_constraint(array, pltpu.VMEM)
+        for array in (cache_keys, cache_values, other_keys, other_values)
+    ]
 
     def attend(arrays, offsets, own):
         count = len(arrays)
-        ids = jnp.stack([(z_index + offset) % requests for offset in offsets]).astype(jnp.int32)
         whole = lambda shape: pl.BlockSpec(shape, lambda h, *_: (0,) * len(shape))
-        cache_spec = pl.BlockSpec((GROUPS * pages, page_len, HDIM), lambda h, *_: (0, 0, h))
+        cache_spec = pl.BlockSpec(memory_space=pltpu.VMEM)
         own_spec = pl.BlockSpec((2, tok_dev, HDIM), lambda h, *_: (0, 0, h))
         return pl.pallas_call(
             functools.partial(
                 attend_kernel,
-                count=count,
+                offsets=tuple(offset % requests for offset in offsets),
                 own=own,
                 pages=pages,
                 page_len=page_len,
@@ -297,38 +303,41 @@
                 out_specs=(whole((chunk, width)),) * count,
                 scratch_shapes=[pltpu.VMEM((count, rows, 128), f32)],
             ),
+            compiler_params=pltpu.CompilerParams(vmem_limit_bytes=20 * 1024 * 1024),
             name="attend",
         )(
             req_group,
             cached_lengths,
-            ids,
+            places,
             bias,
             *arrays,
-            cache_keys,
-            cache_values,
-            other_keys,
-            other_values,
+            *caches,
             *((own_kv, other_kv) if own else ()),
         )
 
+    partials = []
     steps = requests // 2
     below = above = mine
-    arrived = []
+    held, offsets, own = (mine,), (0,), True
     for step in range(1, steps + 1):
+        both = step < requests - step
         below = along_z(below, 1)
-        if step < requests - step:
-            above = along_z(above, -1)
-            arrived.append(((below, above), (-step, step)))
-        else:
-            arrived.append(((below,), (-step,)))
-    partials = list(attend((mine,), (0,), True))
-    for arrays, offsets in arrived:
-        for result, offset in zip(attend(arrays, offsets, False), offsets):
-            partials.append(along_z(result, offset))
+        above = along_z(above, -1) if both else above
+        results = attend(held, offsets, own)
+        if step < steps:
+            below, above, results = lax.optimization_barrier((below, above, results))
+        partials += [
+            along_z(result, offset) if offset else result
+            for result, offset in zip(results, offsets)
+        ]
+        held = (below, above) if both else (below,)
+        offsets, own = ((-step, step) if both else (-step,)), False
+    results = attend(held, offsets, own)
+    partials += [along_z(result, offset) for result, offset in zip(results, offsets)]
     small = jax.ShapeDtypeStruct((tok_dev + STAT_ROWS, width), bf16)
-    keep, send = pl.pallas_call(gather_kernel, out_shape=(small, small), name="gather")(*partials)
+    keep, send = pl.pallas_call(gather_kernel, out_shape=(small, small), compiler_params=SMALL, name="gather")(*partials)
     return pl.pallas_call(
-        last_kernel, out_shape=jax.ShapeDtypeStruct((tok_dev, width), bf16), name="last"
+        last_kernel, out_shape=jax.ShapeDtypeStruct((tok_dev, width), bf16), compiler_params=SMALL, name="last"
     )(keep, across(send, 2))
 
 

time: 136 us -> 122 us (0.90)
  Pallas kernels: 60.2 us -> 46.4 us
  local copies, waits for them, and re-layouts: 7.6 us -> 12 us
  waiting for transfers between devices: 31 us -> 28 us
  other arithmetic: 2.37 us -> 0.08 us
    pallas_call x6, Pallas kernels: 53.3 us -> 43.8 us  [the longest x5 42.8 us: attend(): pl.pallas_call(functools.partial(attend_kernel, offsets=tuple((offset % r...]
    unnamed x39 -> x27, local copies, waits for them, and re-layouts: 5.02 us -> 10.6 us
    ppermute x14, waiting for transfers between devices: 18.7 us -> 14.1 us  [along_z(): return lax.ppermute(array, 'seq', pairs)]
    another operation x4 -> x1, other arithmetic: 2.37 us -> 0.08 us  [on_device(): places = jnp.stack([seq_index, seq_index ^ 1, z_index]).astype(jnp.int32)]
    pallas_call x1, Pallas kernels: 1.86 us -> 0.19 us  [on_device(): pl.pallas_call(functools.partial(norm_kernel, full_width=float(width * tp...]
  transfers between devices with their start and end apart: 20 -> 20, of which waited for: 8 -> 4; matrix products, arithmetic and copies ran while one was open for 4% -> 1% of each run, Pallas kernels for 41% -> 37%
where the time goes in v4:
time: 122 us
  Pallas kernels  46.4 us (38%)
  starting transfers between devices  35 us (29%)
  waiting for transfers between devices  28 us (23%)
  local copies, waits for them, and re-layouts  12 us (10%)
    pallas_call x5, Pallas kernels, attend(): pl.pallas_call(functools.partial(attend_kernel, offsets=tuple((offset % r...  42.8 us
    ppermute x14, starting transfers between devices, along_z(): return lax.ppermute(array, 'seq', pairs)  26 us
    ppermute x14, waiting for transfers between devices, along_z(): return lax.ppermute(array, 'seq', pairs)  14.1 us
    unnamed x27, local copies, waits for them, and re-layouts  10.6 us
    ppermute x5, waiting for transfers between devices, across(): lax.ppermute(array, 'seq', [(index, index ^ bit) for index in range(seq_c...  7.61 us
    all_to_all x1, starting transfers between devices, on_device(): sums = lax.all_to_all(sums, 'tp', split_axis=0, concat_axis=0, tiled=True)  6.93 us
    all_to_all x1, waiting for transfers between devices, on_device(): sums = lax.all_to_all(sums, 'tp', split_axis=0, concat_axis=0, tiled=True)  6.34 us
  transfers between devices with their start and end apart: 20, of which 4 were waited for; matrix products, arithmetic and copies ran while one was open for 1% of the time, Pallas kernels for 37%

profile of v4, /device:TPU:64, one launch (start us, length us, event | category | flops | bytes accessed | tf_op | source)
XLA Modules:
  0.0 121.7 jit_solution(10237428710918772340)
XLA Ops:
  0.0 0.0 collective-permute-start.3
  0.0 0.5 collective-permute-start.4
  0.5 0.9 copy-done.4
  1.4 0.9 copy-done.6
  2.3 0.8 sums.1
  3.1 6.9 %all-to-all-start = ((f32[8,8,128]{2,1,0:T(8,128)}), f32[8,8,128]{2,1,0:T(8,128)S(1)}, u32[]{:S(2)}, u32[]{:S(2)}) async-start(f32[8,8,128]{2,1,0:T(8,128)} %sums.1), calls=%async_computation | async-start | bytes 65536 | tf_op jit(solution)/shard_map/all_to_all | solution.py:253
  10.0 0.7 broadcast_in_dim.6.qg_ref
  10.7 0.7 broadcast_in_dim.7.kg_ref
  11.4 6.3 %all-to-all-done.sums_ref = f32[8,8,128]{2,1,0:T(8,128)S(1)} async-done(((f32[8,8,128]{2,1,0:T(8,128)}), f32[8,8,128]{2,1,0:T(8,128)S(1)}, u32[]{:S(2)}, u32[]{:S(2)}) %all-to-all-start) | async-done | bytes 32800 | tf_op jit(solution)/shard_map/all_to_all | solution.py:253
  17.7 0.9 copy-done.5
  18.6 0.9 copy-done.7
  19.5 0.9 copy-done.8
  20.4 0.2 norm.1
  20.6 0.8 collective-permute-start
  21.3 0.0 collective-permute-start.5
  21.4 3.7 %collective-permute-done = bf16[64,640]{1,0:T(8,128)(2,1)S(1)} collective-permute-done((bf16[64,640]{1,0:T(8,128)(2,1)S(1)}, bf16[64,640]{1,0:T(8,128)(2,1)S(1)}, u32[]{:S(2)}, u32[]{:S(2)}) %collective-permute-start) | collective-permute-done | bytes 81952 | tf_op jit(solution)/shard_map/ppermute | solution.py:248
  25.1 2.0 %collective-permute-start.1 = (bf16[128,640]{1,0:T(8,128)(2,1)S(1)}, bf16[128,640]{1,0:T(8,128)(2,1)S(1)}, u32[]{:S(2)}, u32[]{:S(2)}) collective-permute-start(bf16[128,640]{1,0:T(8,128)(2,1)S(1)} %constant_dynamic-update-slice_fusion.refs_0_), channel_id=1, source_target_pairs={{0,32},{8,40},{16,48},{24,56},{32,64},{40,72},{48,80},{56,88},{64,... | collective-permute-start | bytes 491528 | tf_op jit(solution)/shard_map/ppermute | solution.py:245
  27.1 0.1 collective-permute-start.2
  27.2 0.1 pad_add_fusion.place_ref
  27.3 0.7 copy-done.9
  28.0 0.7 copy-done.12
  28.6 0.7 bias.1.bias_ref
  29.3 0.0 collective-permute-done.5.refs_6_
  29.4 0.0 collective-permute-done.3.refs_3_.refs_4_
  29.4 0.0 copy-start
  29.4 1.7 %copy-done = bf16[16,128,640]{2,1,0:T(8,128)(2,1)S(1)} copy-done((bf16[16,128,640]{2,1,0:T(8,128)(2,1)S(1)}, bf16[16,128,640]{2,1,0:T(8,128)(2,1)}, u32[]{:S(2)}) %copy-start) | copy-done | bytes 2621464
  31.1 1.7 %copy-done.2 = bf16[16,128,640]{2,1,0:T(8,128)(2,1)S(1)} copy-done((bf16[16,128,640]{2,1,0:T(8,128)(2,1)S(1)}, bf16[16,128,640]{2,1,0:T(8,128)(2,1)}, u32[]{:S(2)}) %copy-start.2) | copy-done | bytes 2621464
  32.9 0.7 copy-done.10
  33.5 0.7 copy-done.11
  34.2 6.8 %attend.5.refs_0_ = bf16[136,640]{1,0:T(8,128)(2,1)S(1)} custom-call(s32[8]{0:T(128)S(1)} %copy-done.11, s32[2]{0:T(128)S(1)} %copy-done.10, s32[3]{0:T(128)S(1)} %pad_add_fusion.place_ref, f32[2,1,2048]{2,1,0:T(1,128)S(1)} %bias.1.bias_ref, bf16[128,640]{1,0:T(8,128)(2,1)S(1)} %constant_dynamic-update-slice_fusion.refs_0_, ...), custom_call_target="tpu_custom_call" | custom-call | tf_op jit(solution)/shard_map/attend/pallas_call | solution.py:286
  41.0 3.1 %collective-permute-start.6 = (bf16[128,640]{1,0:T(8,128)(2,1)S(1)}, bf16[128,640]{1,0:T(8,128)(2,1)S(1)}, u32[]{:S(2)}, u32[]{:S(2)}) collective-permute-start(bf16[128,640]{1,0:T(8,128)(2,1)S(1)} %collective-permute-done.1.refs_0_), channel_id=1, source_target_pairs={{0,32},{8,40},{16,48},{24,56},{32,64},{40,72},{48,80},{56,88},{64,... | collective-permute-start | bytes 491528 | tf_op jit(solution)/shard_map/ppermute | solution.py:245
  44.1 9.9 %attend.6 = (bf16[136,640]{1,0:T(8,128)(2,1)S(1)}, bf16[136,640]{1,0:T(8,128)(2,1)S(1)}) custom-call(s32[8]{0:T(128)S(1)} %copy-done.11, s32[2]{0:T(128)S(1)} %copy-done.10, s32[3]{0:T(128)S(1)} %pad_add_fusion.place_ref, f32[2,1,2048]{2,1,0:T(1,128)S(1)} %bias.1.bias_ref, bf16[128,640]{1,0:T(8,128)(2,1)S(1)} %collective-permute-done.1.refs_0_, ...), custom_call_target="tpu_custom_call" | custom-call | tf_op jit(solution)/shard_map/attend/pallas_call | solution.py:286
  54.0 3.4 %collective-permute-start.10 = (bf16[128,640]{1,0:T(8,128)(2,1)S(1)}, bf16[128,640]{1,0:T(8,128)(2,1)S(1)}, u32[]{:S(2)}, u32[]{:S(2)}) collective-permute-start(bf16[128,640]{1,0:T(8,128)(2,1)S(1)} %collective-permute-done.6.refs_0_), channel_id=1, source_target_pairs={{0,32},{8,40},{16,48},{24,56},{32,64},{40,72},{48,80},{56,88},{64,... | collective-permute-start | bytes 491528 | tf_op jit(solution)/shard_map/ppermute | solution.py:245
  57.4 1.2 collective-permute-start.8
  58.6 2.0 %collective-permute-start.9 = (bf16[136,640]{1,0:T(8,128)(2,1)S(1)}, bf16[136,640]{1,0:T(8,128)(2,1)S(1)}, u32[]{:S(2)}, u32[]{:S(2)}) collective-permute-start(bf16[136,640]{1,0:T(8,128)(2,1)S(1)} %get-tuple-element.34), channel_id=1, source_target_pairs={{0,32},{8,40},{16,48},{24,56},{32,64},{40,72},{48,80},{56,88},{64,... | collective-permute-start | bytes 522248 | tf_op jit(solution)/shard_map/ppermute | solution.py:245
  60.6 9.9 %attend.7 = (bf16[136,640]{1,0:T(8,128)(2,1)S(1)}, bf16[136,640]{1,0:T(8,128)(2,1)S(1)}) custom-call(s32[8]{0:T(128)S(1)} %copy-done.11, s32[2]{0:T(128)S(1)} %copy-done.10, s32[3]{0:T(128)S(1)} %pad_add_fusion.place_ref, f32[2,1,2048]{2,1,0:T(1,128)S(1)} %bias.1.bias_ref, bf16[128,640]{1,0:T(8,128)(2,1)S(1)} %collective-permute-done.6.refs_0_, ...), custom_call_target="tpu_custom_call" | custom-call | tf_op jit(solution)/shard_map/attend/pallas_call | solution.py:286
  70.5 3.3 %collective-permute-start.16 = (bf16[128,640]{1,0:T(8,128)(2,1)S(1)}, bf16[128,640]{1,0:T(8,128)(2,1)S(1)}, u32[]{:S(2)}, u32[]{:S(2)}) collective-permute-start(bf16[128,640]{1,0:T(8,128)(2,1)S(1)} %collective-permute-done.10.refs_0_), channel_id=1, source_target_pairs={{0,32},{8,40},{16,48},{24,56},{32,64},{40,72},{48,80},{56,88},{64,... | collective-permute-start | bytes 491528 | tf_op jit(solution)/shard_map/ppermute | solution.py:245
  73.8 4.1 %collective-permute-start.13 = (bf16[136,640]{1,0:T(8,128)(2,1)S(1)}, bf16[136,640]{1,0:T(8,128)(2,1)S(1)}, u32[]{:S(2)}, u32[]{:S(2)}) collective-permute-start(bf16[136,640]{1,0:T(8,128)(2,1)S(1)} %get-tuple-element.40), channel_id=1, source_target_pairs={{0,64},{8,72},{16,80},{24,88},{32,96},{40,104},{48,112},{56,120},{... | collective-permute-start | bytes 522248 | tf_op jit(solution)/shard_map/ppermute | solution.py:245
  78.0 9.9 %attend.8 = (bf16[136,640]{1,0:T(8,128)(2,1)S(1)}, bf16[136,640]{1,0:T(8,128)(2,1)S(1)}) custom-call(s32[8]{0:T(128)S(1)} %copy-done.11, s32[2]{0:T(128)S(1)} %copy-done.10, s32[3]{0:T(128)S(1)} %pad_add_fusion.place_ref, f32[2,1,2048]{2,1,0:T(1,128)S(1)} %bias.1.bias_ref, bf16[128,640]{1,0:T(8,128)(2,1)S(1)} %collective-permute-done.10.refs_0_, ...), custom_call_target="tpu_custom_call" | custom-call | tf_op jit(solution)/shard_map/attend/pallas_call | solution.py:286
  87.9 2.2 %collective-permute-start.14 = (bf16[136,640]{1,0:T(8,128)(2,1)S(1)}, bf16[136,640]{1,0:T(8,128)(2,1)S(1)}, u32[]{:S(2)}, u32[]{:S(2)}) collective-permute-start(bf16[136,640]{1,0:T(8,128)(2,1)S(1)} %get-tuple-element.43), channel_id=1, source_target_pairs={{0,160},{8,168},{16,176},{24,184},{32,192},{40,200},{48,208},{56,2... | collective-permute-start | bytes 522248 | tf_op jit(solution)/shard_map/ppermute | solution.py:245
  90.1 6.2 %attend.9 = bf16[136,640]{1,0:T(8,128)(2,1)S(1)} custom-call(s32[8]{0:T(128)S(1)} %copy-done.11, s32[2]{0:T(128)S(1)} %copy-done.10, s32[3]{0:T(128)S(1)} %pad_add_fusion.place_ref, f32[2,1,2048]{2,1,0:T(1,128)S(1)} %bias.1.bias_ref, bf16[128,640]{1,0:T(8,128)(2,1)S(1)} %collective-permute-done.16.refs_0_, bf16[16,128,640]{2,1,0:T(8,128)(2,1)S(1)} %copy-done.1, ...), custom_call_target="tpu_custom_call" | custom-call | tf_op jit(solution)/shard_map/attend/pallas_call | solution.py:286
  96.4 2.9 %collective-permute-start.15 = (bf16[136,640]{1,0:T(8,128)(2,1)S(1)}, bf16[136,640]{1,0:T(8,128)(2,1)S(1)}, u32[]{:S(2)}, u32[]{:S(2)}) collective-permute-start(bf16[136,640]{1,0:T(8,128)(2,1)S(1)} %get-tuple-element.44), channel_id=1, source_target_pairs={{0,96},{8,104},{16,112},{24,120},{32,128},{40,136},{48,144},{56,15... | collective-permute-start | bytes 522248 | tf_op jit(solution)/shard_map/ppermute | solution.py:245
  99.3 1.7 %collective-permute-start.17 = (bf16[136,640]{1,0:T(8,128)(2,1)S(1)}, bf16[136,640]{1,0:T(8,128)(2,1)S(1)}, u32[]{:S(2)}, u32[]{:S(2)}) collective-permute-start(bf16[136,640]{1,0:T(8,128)(2,1)S(1)} %attend.9), channel_id=1, source_target_pairs={{0,128},{8,136},{16,144},{24,152},{32,160},{40,168},{48,176},{56,1... | collective-permute-start | bytes 522248 | tf_op jit(solution)/shard_map/ppermute | solution.py:245
  101.1 14.1 %collective-permute-done.15.refs_6_ = bf16[136,640]{1,0:T(8,128)(2,1)S(1)} collective-permute-done((bf16[136,640]{1,0:T(8,128)(2,1)S(1)}, bf16[136,640]{1,0:T(8,128)(2,1)S(1)}, u32[]{:S(2)}, u32[]{:S(2)}) %collective-permute-start.15) | collective-permute-done | bytes 174112 | tf_op jit(solution)/shard_map/ppermute | solution.py:245
  115.1 1.0 gather.1
  116.2 0.8 collective-permute-start.18
  116.9 3.9 %collective-permute-done.18.two_ref = bf16[72,640]{1,0:T(8,128)(2,1)S(1)} collective-permute-done((bf16[72,640]{1,0:T(8,128)(2,1)S(1)}, bf16[72,640]{1,0:T(8,128)(2,1)S(1)}, u32[]{:S(2)}, u32[]{:S(2)}) %collective-permute-start.18) | collective-permute-done | bytes 92192 | tf_op jit(solution)/shard_map/ppermute | solution.py:248
  120.8 0.9 last.1
  (33 shorter events, 0.1 us)
Async XLA Ops:
  0.0 29.4 %collective-permute-start.3 = (bf16[16,128,640]{2,1,0:T(8,128)(2,1)}, bf16[16,128,640]{2,1,0:T(8,128)(2,1)S(1)}, u32[]{:S(2)}, u32[]{:S(2)}) collective-permute-start(bf16[16,128,640]{2,1,0:T(8,128)(2,1)} %refs_1_.3), channel_id=1, source_target_pairs={{0,8},{8,0},{16,24},{24,16},{32,40},{40,32},{48,56},{56,48},{64,72... | collective-permute-start | bytes 7864328 | tf_op jit(solution)/shard_map/ppermute | solution.py:248
  0.0 29.4 %collective-permute-start.4 = (bf16[16,128,640]{2,1,0:T(8,128)(2,1)}, bf16[16,128,640]{2,1,0:T(8,128)(2,1)}, u32[]{:S(2)}, u32[]{:S(2)}) collective-permute-start(bf16[16,128,640]{2,1,0:T(8,128)(2,1)} %refs_2_.9), channel_id=1, source_target_pairs={{0,8},{8,0},{16,24},{24,16},{32,40},{40,32},{48,56},{56,48},{64,72... | collective-permute-start | bytes 7864328 | tf_op jit(solution)/shard_map/ppermute | solution.py:248
  0.5 0.9 copy-start.4
  1.4 0.9 copy-start.6
  3.1 14.7 %all-to-all-start = ((f32[8,8,128]{2,1,0:T(8,128)}), f32[8,8,128]{2,1,0:T(8,128)S(1)}, u32[]{:S(2)}, u32[]{:S(2)}) async-start(f32[8,8,128]{2,1,0:T(8,128)} %sums.1), calls=%async_computation | async-start | bytes 65536 | tf_op jit(solution)/shard_map/all_to_all | solution.py:253
  17.7 0.9 copy-start.5
  18.6 0.9 copy-start.7
  19.5 0.9 copy-start.8
  20.6 4.5 %collective-permute-start = (bf16[64,640]{1,0:T(8,128)(2,1)S(1)}, bf16[64,640]{1,0:T(8,128)(2,1)S(1)}, u32[]{:S(2)}, u32[]{:S(2)}) collective-permute-start(bf16[64,640]{1,0:T(8,128)(2,1)S(1)} %get-tuple-element.26), channel_id=1, source_target_pairs={{0,16},{8,24},{16,0},{24,8},{32,48},{40,56},{48,32},{56,40},{64,80... | collective-permute-start | bytes 245768 | tf_op jit(solution)/shard_map/ppermute | solution.py:248
  21.3 8.0 %collective-permute-start.5 = (bf16[2,64,640]{2,1,0:T(8,128)(2,1)S(1)}, bf16[2,64,640]{2,1,0:T(8,128)(2,1)S(1)}, u32[]{:S(2)}, u32[]{:S(2)}) collective-permute-start(bf16[2,64,640]{2,1,0:T(8,128)(2,1)S(1)} %get-tuple-element.27.refs_5_), channel_id=1, source_target_pairs={{0,8},{8,0},{16,24},{24,16},{32,40},{40,32},{48,56},{56,48},{64,72... | collective-permute-start | bytes 491528 | tf_op jit(solution)/shard_map/ppermute | solution.py:248
  25.1 15.8 %collective-permute-start.1 = (bf16[128,640]{1,0:T(8,128)(2,1)S(1)}, bf16[128,640]{1,0:T(8,128)(2,1)S(1)}, u32[]{:S(2)}, u32[]{:S(2)}) collective-permute-start(bf16[128,640]{1,0:T(8,128)(2,1)S(1)} %constant_dynamic-update-slice_fusion.refs_0_), channel_id=1, source_target_pairs={{0,32},{8,40},{16,48},{24,56},{32,64},{40,72},{48,80},{56,88},{64,... | collective-permute-start | bytes 491528 | tf_op jit(solution)/shard_map/ppermute | solution.py:245
  27.1 13.9 %collective-permute-start.2 = (bf16[128,640]{1,0:T(8,128)(2,1)S(1)}, bf16[128,640]{1,0:T(8,128)(2,1)S(1)}, u32[]{:S(2)}, u32[]{:S(2)}) collective-permute-start(bf16[128,640]{1,0:T(8,128)(2,1)S(1)} %constant_dynamic-update-slice_fusion.refs_0_), channel_id=1, source_target_pairs={{0,224},{8,232},{16,240},{24,248},{32,0},{40,8},{48,16},{56,24},{6... | collective-permute-start | bytes 491528 | tf_op jit(solution)/shard_map/ppermute | solution.py:245
  27.3 0.7 copy-start.9
  28.0 0.7 copy-start.12
  29.4 1.7 %copy-start = (bf16[16,128,640]{2,1,0:T(8,128)(2,1)S(1)}, bf16[16,128,640]{2,1,0:T(8,128)(2,1)}, u32[]{:S(2)}) copy-start(bf16[16,128,640]{2,1,0:T(8,128)(2,1)} %refs_1_.3) | copy-start | bytes 7864324
  31.1 1.7 %copy-start.2 = (bf16[16,128,640]{2,1,0:T(8,128)(2,1)S(1)}, bf16[16,128,640]{2,1,0:T(8,128)(2,1)}, u32[]{:S(2)}) copy-start(bf16[16,128,640]{2,1,0:T(8,128)(2,1)} %refs_2_.9) | copy-start | bytes 7864324
  32.9 0.7 copy-start.10
  33.5 0.7 copy-start.11
  34.2 9.9 %copy-start.1 = (bf16[16,128,640]{2,1,0:T(8,128)(2,1)S(1)}, bf16[16,128,640]{2,1,0:T(8,128)(2,1)}, u32[]{:S(2)}) copy-start(bf16[16,128,640]{2,1,0:T(8,128)(2,1)} %refs_1_.3) | copy-start | bytes 7864324
  34.2 9.9 %copy-start.3 = (bf16[16,128,640]{2,1,0:T(8,128)(2,1)S(1)}, bf16[16,128,640]{2,1,0:T(8,128)(2,1)}, u32[]{:S(2)}) copy-start(bf16[16,128,640]{2,1,0:T(8,128)(2,1)} %refs_2_.9) | copy-start | bytes 7864324
  41.0 13.0 %collective-permute-start.6 = (bf16[128,640]{1,0:T(8,128)(2,1)S(1)}, bf16[128,640]{1,0:T(8,128)(2,1)S(1)}, u32[]{:S(2)}, u32[]{:S(2)}) collective-permute-start(bf16[128,640]{1,0:T(8,128)(2,1)S(1)} %collective-permute-done.1.refs_0_), channel_id=1, source_target_pairs={{0,32},{8,40},{16,48},{24,56},{32,64},{40,72},{48,80},{56,88},{64,... | collective-permute-start | bytes 491528 | tf_op jit(solution)/shard_map/ppermute | solution.py:245
  44.1 9.9 %collective-permute-start.7 = (bf16[128,640]{1,0:T(8,128)(2,1)S(1)}, bf16[128,640]{1,0:T(8,128)(2,1)S(1)}, u32[]{:S(2)}, u32[]{:S(2)}) collective-permute-start(bf16[128,640]{1,0:T(8,128)(2,1)S(1)} %collective-permute-done.2.refs_1_), channel_id=1, source_target_pairs={{0,224},{8,232},{16,240},{24,248},{32,0},{40,8},{48,16},{56,24},{6... | collective-permute-start | bytes 491528 | tf_op jit(solution)/shard_map/ppermute | solution.py:245
  54.0 16.5 %collective-permute-start.10 = (bf16[128,640]{1,0:T(8,128)(2,1)S(1)}, bf16[128,640]{1,0:T(8,128)(2,1)S(1)}, u32[]{:S(2)}, u32[]{:S(2)}) collective-permute-start(bf16[128,640]{1,0:T(8,128)(2,1)S(1)} %collective-permute-done.6.refs_0_), channel_id=1, source_target_pairs={{0,32},{8,40},{16,48},{24,56},{32,64},{40,72},{48,80},{56,88},{64,... | collective-permute-start | bytes 491528 | tf_op jit(solution)/shard_map/ppermute | solution.py:245
  57.4 13.2 %collective-permute-start.11 = (bf16[128,640]{1,0:T(8,128)(2,1)S(1)}, bf16[128,640]{1,0:T(8,128)(2,1)S(1)}, u32[]{:S(2)}, u32[]{:S(2)}) collective-permute-start(bf16[128,640]{1,0:T(8,128)(2,1)S(1)} %collective-permute-done.7.refs_1_), channel_id=1, source_target_pairs={{0,224},{8,232},{16,240},{24,248},{32,0},{40,8},{48,16},{56,24},{6... | collective-permute-start | bytes 491528 | tf_op jit(solution)/shard_map/ppermute | solution.py:245
  57.4 39.0 %collective-permute-start.8 = (bf16[136,640]{1,0:T(8,128)(2,1)S(1)}, bf16[136,640]{1,0:T(8,128)(2,1)S(1)}, u32[]{:S(2)}, u32[]{:S(2)}) collective-permute-start(bf16[136,640]{1,0:T(8,128)(2,1)S(1)} %get-tuple-element.33), channel_id=1, source_target_pairs={{0,224},{8,232},{16,240},{24,248},{32,0},{40,8},{48,16},{56,24},{6... | collective-permute-start | bytes 522248 | tf_op jit(solution)/shard_map/ppermute | solution.py:245
  58.6 40.8 %collective-permute-start.9 = (bf16[136,640]{1,0:T(8,128)(2,1)S(1)}, bf16[136,640]{1,0:T(8,128)(2,1)S(1)}, u32[]{:S(2)}, u32[]{:S(2)}) collective-permute-start(bf16[136,640]{1,0:T(8,128)(2,1)S(1)} %get-tuple-element.34), channel_id=1, source_target_pairs={{0,32},{8,40},{16,48},{24,56},{32,64},{40,72},{48,80},{56,88},{64,... | collective-permute-start | bytes 522248 | tf_op jit(solution)/shard_map/ppermute | solution.py:245
  70.5 17.4 %collective-permute-start.16 = (bf16[128,640]{1,0:T(8,128)(2,1)S(1)}, bf16[128,640]{1,0:T(8,128)(2,1)S(1)}, u32[]{:S(2)}, u32[]{:S(2)}) collective-permute-start(bf16[128,640]{1,0:T(8,128)(2,1)S(1)} %collective-permute-done.10.refs_0_), channel_id=1, source_target_pairs={{0,32},{8,40},{16,48},{24,56},{32,64},{40,72},{48,80},{56,88},{64,... | collective-permute-start | bytes 491528 | tf_op jit(solution)/shard_map/ppermute | solution.py:245
  73.8 27.2 %collective-permute-start.12 = (bf16[136,640]{1,0:T(8,128)(2,1)S(1)}, bf16[136,640]{1,0:T(8,128)(2,1)S(1)}, u32[]{:S(2)}, u32[]{:S(2)}) collective-permute-start(bf16[136,640]{1,0:T(8,128)(2,1)S(1)} %get-tuple-element.39), channel_id=1, source_target_pairs={{0,192},{8,200},{16,208},{24,216},{32,224},{40,232},{48,240},{56,2... | collective-permute-start | bytes 522248 | tf_op jit(solution)/shard_map/ppermute | solution.py:245
  73.8 27.2 %collective-permute-start.13 = (bf16[136,640]{1,0:T(8,128)(2,1)S(1)}, bf16[136,640]{1,0:T(8,128)(2,1)S(1)}, u32[]{:S(2)}, u32[]{:S(2)}) collective-permute-start(bf16[136,640]{1,0:T(8,128)(2,1)S(1)} %get-tuple-element.40), channel_id=1, source_target_pairs={{0,64},{8,72},{16,80},{24,88},{32,96},{40,104},{48,112},{56,120},{... | collective-permute-start | bytes 522248 | tf_op jit(solution)/shard_map/ppermute | solution.py:245
  87.9 13.1 %collective-permute-start.14 = (bf16[136,640]{1,0:T(8,128)(2,1)S(1)}, bf16[136,640]{1,0:T(8,128)(2,1)S(1)}, u32[]{:S(2)}, u32[]{:S(2)}) collective-permute-start(bf16[136,640]{1,0:T(8,128)(2,1)S(1)} %get-tuple-element.43), channel_id=1, source_target_pairs={{0,160},{8,168},{16,176},{24,184},{32,192},{40,200},{48,208},{56,2... | collective-permute-start | bytes 522248 | tf_op jit(solution)/shard_map/ppermute | solution.py:245
  96.4 18.7 %collective-permute-start.15 = (bf16[136,640]{1,0:T(8,128)(2,1)S(1)}, bf16[136,640]{1,0:T(8,128)(2,1)S(1)}, u32[]{:S(2)}, u32[]{:S(2)}) collective-permute-start(bf16[136,640]{1,0:T(8,128)(2,1)S(1)} %get-tuple-element.44), channel_id=1, source_target_pairs={{0,96},{8,104},{16,112},{24,120},{32,128},{40,136},{48,144},{56,15... | collective-permute-start | bytes 522248 | tf_op jit(solution)/shard_map/ppermute | solution.py:245
  99.3 15.8 %collective-permute-start.17 = (bf16[136,640]{1,0:T(8,128)(2,1)S(1)}, bf16[136,640]{1,0:T(8,128)(2,1)S(1)}, u32[]{:S(2)}, u32[]{:S(2)}) collective-permute-start(bf16[136,640]{1,0:T(8,128)(2,1)S(1)} %attend.9), channel_id=1, source_target_pairs={{0,128},{8,136},{16,144},{24,152},{32,160},{40,168},{48,176},{56,1... | collective-permute-start | bytes 522248 | tf_op jit(solution)/shard_map/ppermute | solution.py:245
  116.2 4.6 %collective-permute-start.18 = (bf16[72,640]{1,0:T(8,128)(2,1)S(1)}, bf16[72,640]{1,0:T(8,128)(2,1)S(1)}, u32[]{:S(2)}, u32[]{:S(2)}) collective-permute-start(bf16[72,640]{1,0:T(8,128)(2,1)S(1)} %get-tuple-element.46), channel_id=1, source_target_pairs={{0,16},{8,24},{16,0},{24,8},{32,48},{40,56},{48,32},{56,40},{64,80... | collective-permute-start | bytes 276488 | tf_op jit(solution)/shard_map/ppermute | solution.py:248
